TPU v7x, 128 devices: a whole 4x4x4 slice. The times are simulated.
128 devices in a mesh: tm: 4 (over z_hi, core), space: 32 (over x, y, z_lo).
Axes of the slice: x: 4, y: 4, z: 4 (z_hi: 2, z_lo: 2; z = z_hi * 2 + z_lo), core: 2. Of those that a mesh axis runs over, the one named last changes fastest.
Arguments:
- initial: bfloat16 [135, 4096], P(None, 'space'), may hold values from -6 to 6
- forcing: bfloat16 [64, 135, 4096], P('tm', None, 'space'), may hold values from -2 to 2
- damping: float32 [4096], P('space'), may hold values from 0.003 to 0.1
- block_inv: bfloat16 [2, 135, 135], replicated, as said below
- coarse_inv: bfloat16 [2, 135, 135], replicated, as said below
- coupling: bfloat16 [6, 135, 135], replicated, may hold values from -0.078125 to 0.078125
- etype: int32 [32], P('space'), may hold values from 0 to 1
- send_index: int32 [4096], P('space'), may hold values from 0 to 127
- conn: int32 [6, 4096], P(None, 'space'), may hold values from 0 to 255
Outputs:
- states: bfloat16 [64, 135, 4096], P('tm', None, 'space')
Inputs may be any that keep to these rules, and one draw needn't show every extreme that they name: block_inv[0] is the inverse of a hexahedron's diagonal block, block_inv[1] that of a prism, with zero rows and columns from 90 on. coarse_inv[0] is the inverse of a hexahedron's coarse diagonal block, coarse_inv[1] that of a prism, with zero rows and columns from 90 on. `send_index`: the first 64 entries of a partition's list name the elements it sends to the partition before, the last 64 those it sends to the partition after. `conn`: entries below 128 name an element of the same partition; the next 64 name the columns received from the partition before, the last 64 those received from the partition after.
All inputs are finite; a program needn't handle non-finite values.
Results may differ from a plain program's by a relative error of at most 0.018.
Values may be sent and summed in bfloat16 or wider, within the bound.
A program may use at most 64 MiB of HBM per device.

v0:
```python
import jax
import jax.numpy as jnp
from jax import lax
from jax.sharding import PartitionSpec as P

PRISM = 90
SWEEPS = 2
COARSEN = 4


def padded(cells, sides, width):
    for axis, dim in sides:
        count = lax.axis_size(axis)
        ends = count - 1
        head = lax.slice_in_dim(cells, 0, width, axis=dim)
        tail = lax.slice_in_dim(cells, cells.shape[dim] - width, cells.shape[dim], axis=dim)
        cells = jnp.concatenate(
            [
                lax.ppermute(tail, axis, [(i, (i + 1) % count) for i in range(ends)]),
                cells,
                lax.ppermute(head, axis, [((i + 1) % count, i) for i in range(ends)]),
            ],
            axis=dim,
        )
    return cells


def passed_along(array, axis, by):
    size = lax.axis_size(axis)
    pairs = [(i, i + by) for i in range(size) if 0 <= i + by < size]
    return lax.ppermute(array, axis, pairs)


def shards(initial, forcing, damping, block_inv, coarse_inv, coupling, etype, send_index, conn):
    width_rows = initial.shape[0]
    local_elems = initial.shape[1]
    block_count = etype.shape[0]
    block_length = local_elems // block_count
    halo_length = send_index.shape[0] // 2
    face_count = conn.shape[0]
    interval_count = forcing.shape[0] // COARSEN
    element_kinds = jnp.broadcast_to(etype[:, None], (block_count, block_length)).reshape(
        local_elems
    )
    face_rows = lax.broadcasted_iota(jnp.int32, (face_count, local_elems), 0)
    face_keep = (
        ((face_rows < face_count - 1) | (element_kinds[None, :] == 0))
        .astype(jnp.bfloat16)
        .reshape(-1)
    )
    conn_flat = conn.reshape(-1)
    rows_iota = lax.broadcasted_iota(jnp.int32, (width_rows, local_elems), 0)
    valid_rows = (rows_iota < PRISM) | (element_kinds[None, :] == 0)
    start_field = jnp.where(valid_rows, initial, jnp.zeros_like(initial))
    is_hex = (etype == 0)[:, None, None]
    fine_chosen = jnp.where(is_hex, block_inv[0][None], block_inv[1][None])
    coarse_chosen = jnp.where(is_hex, coarse_inv[0][None], coarse_inv[1][None])
    decay_rate = jnp.exp(-damping)
    coarse_decay = jnp.exp(-COARSEN * damping)

    def neighbours(iterate):
        batch_count = iterate.shape[0]
        outgoing = jnp.take(iterate, send_index, axis=2)
        received = padded(outgoing, (("space", 2),), halo_length)
        extended = jnp.concatenate(
            [iterate, received[:, :, :halo_length], received[:, :, 3 * halo_length :]], axis=2
        )
        gathered = jnp.take(extended, conn_flat, axis=2) * face_keep
        return gathered.reshape(batch_count, width_rows, face_count, local_elems)

    def propagate(start_states, drive_term, chosen):
        batch_count = start_states.shape[0]
        iterate = start_states
        for sweep_index in range(SWEEPS):
            coupled = jnp.einsum(
                "fij,njfk->nik", coupling, neighbours(iterate), preferred_element_type=jnp.float32
            )
            rhs_value = (drive_term - coupled).astype(jnp.bfloat16)
            blocked = rhs_value.reshape(batch_count, width_rows, block_count, block_length)
            applied = jnp.einsum(
                "bij,njbk->nibk", chosen, blocked, preferred_element_type=jnp.float32
            )
            iterate = applied.reshape(batch_count, width_rows, local_elems).astype(jnp.bfloat16)
        return iterate

    forcing_view = forcing.reshape(interval_count, COARSEN, width_rows, local_elems)

    def fine_step(states_now, step_index):
        drive_term = decay_rate * states_now.astype(jnp.float32) + forcing_view[
            :, step_index
        ].astype(jnp.float32)
        return propagate(states_now, drive_term, fine_chosen)

    first_device = lax.axis_index("tm") == 0
    leading = jnp.where(first_device, start_field, jnp.zeros_like(start_field))[None]
    zero_rest = jnp.zeros((interval_count - 1, width_rows, local_elems), jnp.bfloat16)
    states_now = jnp.concatenate([leading, zero_rest], axis=0)
    for step_index in range(COARSEN):
        states_now = fine_step(states_now, step_index)
    residuals = states_now
    device_count = lax.axis_size("tm")
    incoming = jnp.zeros((1, width_rows, local_elems), jnp.bfloat16)
    collected = []
    for turn_index in range(device_count):
        carried = incoming
        collected = []
        for interval_index in range(interval_count):
            coarse_drive_term = coarse_decay * carried.astype(jnp.float32)
            propagated = propagate(carried, coarse_drive_term, coarse_chosen)
            carried = (
                propagated.astype(jnp.float32)
                + residuals[interval_index : interval_index + 1].astype(jnp.float32)
            ).astype(jnp.bfloat16)
            collected.append(carried)
        if turn_index + 1 < device_count:
            incoming = passed_along(carried, "tm", 1)
    coarse_values = jnp.concatenate(collected, axis=0)
    leading = jnp.where(first_device, start_field[None], incoming)
    states_now = jnp.concatenate([leading, coarse_values[:-1]], axis=0)
    produced = []
    for step_index in range(COARSEN - 1):
        states_now = fine_step(states_now, step_index)
        produced.append(states_now)
    produced.append(coarse_values)
    return jnp.stack(produced, axis=1).reshape(forcing.shape[0], width_rows, local_elems)


def solution(mesh):
    in_specs = (
        P(None, "space"),
        P("tm", None, "space"),
        P("space"),
        P(),
        P(),
        P(),
        P("space"),
        P("space"),
        P(None, "space"),
    )
    out_specs = P("tm", None, "space")
    return jax.shard_map(shards, mesh=mesh, in_specs=in_specs, out_specs=out_specs, check_vma=False)
```

profile of v0, /device:TPU:122, one launch (start us, length us, event | category | flops | bytes accessed | tf_op | source)
XLA Modules:
  0.0 812.6 jit_solution(784744735408562518)
XLA Ops:
  11.4 5.9 collective-permute-start
  30.3 6.9 collective-permute-start.6
  63.7 6.1 collective-permute-done.9
  129.5 4.9 collective-permute-start.2
  146.4 6.9 collective-permute-start.16
  159.0 4.3 collective-permute-done.17
  180.3 5.6 collective-permute-done.19
  202.1 4.9 collective-permute-done.21
  213.6 4.3 collective-permute-start.23
  218.0 4.5 collective-permute-done.23
  233.1 4.9 collective-permute-done.25
  248.7 4.9 collective-permute-done.27
  264.2 4.9 collective-permute-done.29
  279.7 4.9 collective-permute-done.31
  290.1 4.8 collective-permute-done.32
  302.0 4.9 collective-permute-done.34
  317.7 4.7 collective-permute-done.36
  333.1 4.9 collective-permute-done.38
  348.6 4.9 collective-permute-done.40
  364.2 4.9 collective-permute-done.42
  379.7 4.9 collective-permute-done.44
  395.3 4.9 collective-permute-done.46
  411.0 4.7 collective-permute-done.48
  421.2 5.0 collective-permute-done.49
  433.6 4.6 collective-permute-done.51
  448.8 4.9 collective-permute-done.53
  464.3 4.9 collective-permute-done.55
  479.8 4.9 collective-permute-done.57
  495.4 4.9 collective-permute-done.59
  507.0 4.3 collective-permute-start.61
  511.3 4.5 collective-permute-done.61
  526.4 4.9 collective-permute-done.63
  542.0 4.9 collective-permute-done.65
  552.4 4.8 collective-permute-done.66
  564.3 4.9 collective-permute-done.68
  579.8 4.9 collective-permute-done.70
  595.3 4.9 collective-permute-done.72
  611.0 4.7 collective-permute-done.74
  626.4 4.9 collective-permute-done.76
  641.9 4.9 collective-permute-done.78
  657.5 4.9 collective-permute-done.92
  673.1 4.8 collective-permute-done.94
  690.6 4.9 collective-permute-done.80
  712.2 5.0 collective-permute-done.82
  733.7 5.0 collective-permute-done.84
  755.1 5.2 collective-permute-done.86
  776.7 4.9 collective-permute-done.88
  798.1 4.9 collective-permute-done.90
  (698 shorter events, 568.3 us)
Async XLA Ops:
  4.4 16.4 %collective-permute-start.4 = (bf16[4,135,64]{2,1,0:T(8,128)(2,1)S(1)}, bf16[4,135,64]{2,1,0:T(8,128)(2,1)S(1)}, u32[]{:S(2)}, u32[]{:S(2)}) collective-permute-start(bf16[4,135,64]{2,1,0:T(8,128)(2,1)S(1)} %get-tuple-element.35), channel_id=1, source_target_pairs={{0,1},{1,2},{2,3},{3,4},{4,5},{5,6},{6,7},{7,8},{8,9},{9,10},{10,1... | collective-permute-start | bytes 207368 | tf_op jit(solution)/shard_map/ppermute | solution.py:19
  7.4 13.4 %collective-permute-start.5 = (bf16[4,135,64]{2,1,0:T(8,128)(2,1)S(1)}, bf16[4,135,64]{2,1,0:T(8,128)(2,1)S(1)}, u32[]{:S(2)}, u32[]{:S(2)}) collective-permute-start(bf16[4,135,64]{2,1,0:T(8,128)(2,1)S(1)} %get-tuple-element.36), channel_id=1, source_target_pairs={{1,0},{2,1},{3,2},{4,3},{5,4},{6,5},{7,6},{8,7},{9,8},{10,9},{11,1... | collective-permute-start | bytes 207368 | tf_op jit(solution)/shard_map/ppermute | solution.py:21
  11.4 27.8 %collective-permute-start = (bf16[1,135,64]{1,2,0:T(8,128)(2,1)S(1)}, bf16[1,135,64]{1,2,0:T(8,128)(2,1)S(1)}, u32[]{:S(2)}, u32[]{:S(2)}) collective-permute-start(bf16[1,135,64]{1,2,0:T(8,128)(2,1)S(1)} %get-tuple-element.43), channel_id=1, source_target_pairs={{0,1},{1,2},{2,3},{3,4},{4,5},{5,6},{6,7},{7,8},{8,9},{9,10},{10,1... | collective-permute-start | bytes 51848 | tf_op jit(solution)/shard_map/ppermute | solution.py:19
  17.3 21.9 %collective-permute-start.1 = (bf16[1,135,64]{1,2,0:T(8,128)(2,1)S(1)}, bf16[1,135,64]{1,2,0:T(8,128)(2,1)}, u32[]{:S(2)}, u32[]{:S(2)}) collective-permute-start(bf16[1,135,64]{1,2,0:T(8,128)(2,1)S(1)} %get-tuple-element.44), channel_id=1, source_target_pairs={{1,0},{2,1},{3,2},{4,3},{5,4},{6,5},{7,6},{8,7},{9,8},{10,9},{11,1... | collective-permute-start | bytes 51848 | tf_op jit(solution)/shard_map/ppermute | solution.py:21
  30.3 13.0 %collective-permute-start.6 = (bf16[4,135,64]{2,1,0:T(8,128)(2,1)S(1)}, bf16[4,135,64]{2,1,0:T(8,128)(2,1)S(1)}, u32[]{:S(2)}, u32[]{:S(2)}) collective-permute-start(bf16[4,135,64]{2,1,0:T(8,128)(2,1)S(1)} %get-tuple-element.33), channel_id=1, source_target_pairs={{0,1},{1,2},{2,3},{3,4},{4,5},{5,6},{6,7},{7,8},{8,9},{9,10},{10,1... | collective-permute-start | bytes 207368 | tf_op jit(solution)/shard_map/ppermute | solution.py:19
  37.3 10.0 %collective-permute-start.7 = (bf16[4,135,64]{2,1,0:T(8,128)(2,1)S(1)}, bf16[4,135,64]{2,1,0:T(8,128)(2,1)S(1)}, u32[]{:S(2)}, u32[]{:S(2)}) collective-permute-start(bf16[4,135,64]{2,1,0:T(8,128)(2,1)S(1)} %get-tuple-element.34), channel_id=1, source_target_pairs={{1,0},{2,1},{3,2},{4,3},{5,4},{6,5},{7,6},{8,7},{9,8},{10,9},{11,1... | collective-permute-start | bytes 207368 | tf_op jit(solution)/shard_map/ppermute | solution.py:21
  59.8 10.0 %collective-permute-start.9 = (bf16[4,135,64]{2,1,0:T(8,128)(2,1)S(1)}, bf16[4,135,64]{2,1,0:T(8,128)(2,1)S(1)}, u32[]{:S(2)}, u32[]{:S(2)}) collective-permute-start(bf16[4,135,64]{2,1,0:T(8,128)(2,1)S(1)} %get-tuple-element.32), channel_id=1, source_target_pairs={{1,0},{2,1},{3,2},{4,3},{5,4},{6,5},{7,6},{8,7},{9,8},{10,9},{11,1... | collective-permute-start | bytes 207368 | tf_op jit(solution)/shard_map/ppermute | solution.py:21
  81.7 10.0 %collective-permute-start.11 = (bf16[4,135,64]{2,1,0:T(8,128)(2,1)S(1)}, bf16[4,135,64]{2,1,0:T(8,128)(2,1)S(1)}, u32[]{:S(2)}, u32[]{:S(2)}) collective-permute-start(bf16[4,135,64]{2,1,0:T(8,128)(2,1)S(1)} %get-tuple-element.30), channel_id=1, source_target_pairs={{1,0},{2,1},{3,2},{4,3},{5,4},{6,5},{7,6},{8,7},{9,8},{10,9},{11,1... | collective-permute-start | bytes 207368 | tf_op jit(solution)/shard_map/ppermute | solution.py:21
  103.6 10.0 %collective-permute-start.13 = (bf16[4,135,64]{2,1,0:T(8,128)(2,1)S(1)}, bf16[4,135,64]{2,1,0:T(8,128)(2,1)S(1)}, u32[]{:S(2)}, u32[]{:S(2)}) collective-permute-start(bf16[4,135,64]{2,1,0:T(8,128)(2,1)S(1)} %get-tuple-element.28), channel_id=1, source_target_pairs={{1,0},{2,1},{3,2},{4,3},{5,4},{6,5},{7,6},{8,7},{9,8},{10,9},{11,1... | collective-permute-start | bytes 207368 | tf_op jit(solution)/shard_map/ppermute | solution.py:21
  123.6 12.8 %collective-permute-start.14 = (bf16[4,135,64]{2,1,0:T(8,128)(2,1)S(1)}, bf16[4,135,64]{2,1,0:T(8,128)(2,1)S(1)}, u32[]{:S(2)}, u32[]{:S(2)}) collective-permute-start(bf16[4,135,64]{2,1,0:T(8,128)(2,1)S(1)} %get-tuple-element.25), channel_id=1, source_target_pairs={{0,1},{1,2},{2,3},{3,4},{4,5},{5,6},{6,7},{7,8},{8,9},{9,10},{10,1... | collective-permute-start | bytes 207368 | tf_op jit(solution)/shard_map/ppermute | solution.py:19
  125.5 10.9 %collective-permute-start.15 = (bf16[4,135,64]{2,1,0:T(8,128)(2,1)S(1)}, bf16[4,135,64]{2,1,0:T(8,128)(2,1)S(1)}, u32[]{:S(2)}, u32[]{:S(2)}) collective-permute-start(bf16[4,135,64]{2,1,0:T(8,128)(2,1)S(1)} %get-tuple-element.26), channel_id=1, source_target_pairs={{1,0},{2,1},{3,2},{4,3},{5,4},{6,5},{7,6},{8,7},{9,8},{10,9},{11,1... | collective-permute-start | bytes 207368 | tf_op jit(solution)/shard_map/ppermute | solution.py:21
  129.5 26.0 %collective-permute-start.2 = (bf16[1,135,64]{2,1,0:T(8,128)(2,1)S(1)}, bf16[1,135,64]{2,1,0:T(8,128)(2,1)S(1)}, u32[]{:S(2)}, u32[]{:S(2)}) collective-permute-start(bf16[1,135,64]{2,1,0:T(8,128)(2,1)S(1)} %get-tuple-element.105), channel_id=1, source_target_pairs={{0,1},{1,2},{2,3},{3,4},{4,5},{5,6},{6,7},{7,8},{8,9},{9,10},{10,1... | collective-permute-start | bytes 51848 | tf_op jit(solution)/shard_map/ppermute | solution.py:19
  134.4 21.1 %collective-permute-start.3 = (bf16[1,135,64]{2,1,0:T(8,128)(2,1)S(1)}, bf16[1,135,64]{2,1,0:T(8,128)(2,1)S(1)}, u32[]{:S(2)}, u32[]{:S(2)}) collective-permute-start(bf16[1,135,64]{2,1,0:T(8,128)(2,1)S(1)} %get-tuple-element.106), channel_id=1, source_target_pairs={{1,0},{2,1},{3,2},{4,3},{5,4},{6,5},{7,6},{8,7},{9,8},{10,9},{11,1... | collective-permute-start | bytes 51848 | tf_op jit(solution)/shard_map/ppermute | solution.py:21
  146.4 12.6 %collective-permute-start.16 = (bf16[4,135,64]{2,1,0:T(8,128)(2,1)S(1)}, bf16[4,135,64]{2,1,0:T(8,128)(2,1)S(1)}, u32[]{:S(2)}, u32[]{:S(2)}) collective-permute-start(bf16[4,135,64]{2,1,0:T(8,128)(2,1)S(1)} %get-tuple-element.23), channel_id=1, source_target_pairs={{0,1},{1,2},{2,3},{3,4},{4,5},{5,6},{6,7},{7,8},{8,9},{9,10},{10,1... | collective-permute-start | bytes 207368 | tf_op jit(solution)/shard_map/ppermute | solution.py:19
  153.4 10.0 %collective-permute-start.17 = (bf16[4,135,64]{2,1,0:T(8,128)(2,1)S(1)}, bf16[4,135,64]{2,1,0:T(8,128)(2,1)S(1)}, u32[]{:S(2)}, u32[]{:S(2)}) collective-permute-start(bf16[4,135,64]{2,1,0:T(8,128)(2,1)S(1)} %get-tuple-element.24), channel_id=1, source_target_pairs={{1,0},{2,1},{3,2},{4,3},{5,4},{6,5},{7,6},{8,7},{9,8},{10,9},{11,1... | collective-permute-start | bytes 207368 | tf_op jit(solution)/shard_map/ppermute | solution.py:21
  176.0 10.0 %collective-permute-start.19 = (bf16[4,135,64]{2,1,0:T(8,128)(2,1)S(1)}, bf16[4,135,64]{2,1,0:T(8,128)(2,1)S(1)}, u32[]{:S(2)}, u32[]{:S(2)}) collective-permute-start(bf16[4,135,64]{2,1,0:T(8,128)(2,1)S(1)} %get-tuple-element.22), channel_id=1, source_target_pairs={{1,0},{2,1},{3,2},{4,3},{5,4},{6,5},{7,6},{8,7},{9,8},{10,9},{11,1... | collective-permute-start | bytes 207368 | tf_op jit(solution)/shard_map/ppermute | solution.py:21
  198.1 8.8 %collective-permute-start.21 = (bf16[1,135,64]{2,1,0:T(8,128)(2,1)S(1)}, bf16[1,135,64]{2,1,0:T(8,128)(2,1)S(1)}, u32[]{:S(2)}, u32[]{:S(2)}) collective-permute-start(bf16[1,135,64]{2,1,0:T(8,128)(2,1)S(1)} %get-tuple-element.104), channel_id=1, source_target_pairs={{1,0},{2,1},{3,2},{4,3},{5,4},{6,5},{7,6},{8,7},{9,8},{10,9},{11,1... | collective-permute-start | bytes 51848 | tf_op jit(solution)/shard_map/ppermute | solution.py:21
  213.6 8.8 %collective-permute-start.23 = (bf16[1,135,64]{2,1,0:T(8,128)(2,1)S(1)}, bf16[1,135,64]{2,1,0:T(8,128)(2,1)S(1)}, u32[]{:S(2)}, u32[]{:S(2)}) collective-permute-start(bf16[1,135,64]{2,1,0:T(8,128)(2,1)S(1)} %get-tuple-element.102), channel_id=1, source_target_pairs={{1,0},{2,1},{3,2},{4,3},{5,4},{6,5},{7,6},{8,7},{9,8},{10,9},{11,1... | collective-permute-start | bytes 51848 | tf_op jit(solution)/shard_map/ppermute | solution.py:21
  229.2 8.8 %collective-permute-start.25 = (bf16[1,135,64]{2,1,0:T(8,128)(2,1)S(1)}, bf16[1,135,64]{2,1,0:T(8,128)(2,1)S(1)}, u32[]{:S(2)}, u32[]{:S(2)}) collective-permute-start(bf16[1,135,64]{2,1,0:T(8,128)(2,1)S(1)} %get-tuple-element.100), channel_id=1, source_target_pairs={{1,0},{2,1},{3,2},{4,3},{5,4},{6,5},{7,6},{8,7},{9,8},{10,9},{11,1... | collective-permute-start | bytes 51848 | tf_op jit(solution)/shard_map/ppermute | solution.py:21
  244.7 8.8 %collective-permute-start.27 = (bf16[1,135,64]{2,1,0:T(8,128)(2,1)S(1)}, bf16[1,135,64]{2,1,0:T(8,128)(2,1)S(1)}, u32[]{:S(2)}, u32[]{:S(2)}) collective-permute-start(bf16[1,135,64]{2,1,0:T(8,128)(2,1)S(1)} %get-tuple-element.98), channel_id=1, source_target_pairs={{1,0},{2,1},{3,2},{4,3},{5,4},{6,5},{7,6},{8,7},{9,8},{10,9},{11,1... | collective-permute-start | bytes 51848 | tf_op jit(solution)/shard_map/ppermute | solution.py:21
  260.3 8.8 %collective-permute-start.29 = (bf16[1,135,64]{2,1,0:T(8,128)(2,1)S(1)}, bf16[1,135,64]{2,1,0:T(8,128)(2,1)S(1)}, u32[]{:S(2)}, u32[]{:S(2)}) collective-permute-start(bf16[1,135,64]{2,1,0:T(8,128)(2,1)S(1)} %get-tuple-element.96), channel_id=1, source_target_pairs={{1,0},{2,1},{3,2},{4,3},{5,4},{6,5},{7,6},{8,7},{9,8},{10,9},{11,1... | collective-permute-start | bytes 51848 | tf_op jit(solution)/shard_map/ppermute | solution.py:21
  275.8 8.8 %collective-permute-start.31 = (bf16[1,135,64]{2,1,0:T(8,128)(2,1)S(1)}, bf16[1,135,64]{2,1,0:T(8,128)(2,1)S(1)}, u32[]{:S(2)}, u32[]{:S(2)}) collective-permute-start(bf16[1,135,64]{2,1,0:T(8,128)(2,1)S(1)} %get-tuple-element.94), channel_id=1, source_target_pairs={{1,0},{2,1},{3,2},{4,3},{5,4},{6,5},{7,6},{8,7},{9,8},{10,9},{11,1... | collective-permute-start | bytes 51848 | tf_op jit(solution)/shard_map/ppermute | solution.py:21
  298.1 8.8 %collective-permute-start.34 = (bf16[1,135,64]{2,1,0:T(8,128)(2,1)S(1)}, bf16[1,135,64]{2,1,0:T(8,128)(2,1)S(1)}, u32[]{:S(2)}, u32[]{:S(2)}) collective-permute-start(bf16[1,135,64]{2,1,0:T(8,128)(2,1)S(1)} %get-tuple-element.92), channel_id=1, source_target_pairs={{1,0},{2,1},{3,2},{4,3},{5,4},{6,5},{7,6},{8,7},{9,8},{10,9},{11,1... | collective-permute-start | bytes 51848 | tf_op jit(solution)/shard_map/ppermute | solution.py:21
  313.6 8.8 %collective-permute-start.36 = (bf16[1,135,64]{2,1,0:T(8,128)(2,1)S(1)}, bf16[1,135,64]{2,1,0:T(8,128)(2,1)S(1)}, u32[]{:S(2)}, u32[]{:S(2)}) collective-permute-start(bf16[1,135,64]{2,1,0:T(8,128)(2,1)S(1)} %get-tuple-element.90), channel_id=1, source_target_pairs={{1,0},{2,1},{3,2},{4,3},{5,4},{6,5},{7,6},{8,7},{9,8},{10,9},{11,1... | collective-permute-start | bytes 51848 | tf_op jit(solution)/shard_map/ppermute | solution.py:21
  329.2 8.8 %collective-permute-start.38 = (bf16[1,135,64]{2,1,0:T(8,128)(2,1)S(1)}, bf16[1,135,64]{2,1,0:T(8,128)(2,1)S(1)}, u32[]{:S(2)}, u32[]{:S(2)}) collective-permute-start(bf16[1,135,64]{2,1,0:T(8,128)(2,1)S(1)} %get-tuple-element.88), channel_id=1, source_target_pairs={{1,0},{2,1},{3,2},{4,3},{5,4},{6,5},{7,6},{8,7},{9,8},{10,9},{11,1... | collective-permute-start | bytes 51848 | tf_op jit(solution)/shard_map/ppermute | solution.py:21
  344.7 8.8 %collective-permute-start.40 = (bf16[1,135,64]{2,1,0:T(8,128)(2,1)S(1)}, bf16[1,135,64]{2,1,0:T(8,128)(2,1)S(1)}, u32[]{:S(2)}, u32[]{:S(2)}) collective-permute-start(bf16[1,135,64]{2,1,0:T(8,128)(2,1)S(1)} %get-tuple-element.86), channel_id=1, source_target_pairs={{1,0},{2,1},{3,2},{4,3},{5,4},{6,5},{7,6},{8,7},{9,8},{10,9},{11,1... | collective-permute-start | bytes 51848 | tf_op jit(solution)/shard_map/ppermute | solution.py:21
  360.2 8.8 %collective-permute-start.42 = (bf16[1,135,64]{2,1,0:T(8,128)(2,1)S(1)}, bf16[1,135,64]{2,1,0:T(8,128)(2,1)S(1)}, u32[]{:S(2)}, u32[]{:S(2)}) collective-permute-start(bf16[1,135,64]{2,1,0:T(8,128)(2,1)S(1)} %get-tuple-element.84), channel_id=1, source_target_pairs={{1,0},{2,1},{3,2},{4,3},{5,4},{6,5},{7,6},{8,7},{9,8},{10,9},{11,1... | collective-permute-start | bytes 51848 | tf_op jit(solution)/shard_map/ppermute | solution.py:21
  375.8 8.8 %collective-permute-start.44 = (bf16[1,135,64]{2,1,0:T(8,128)(2,1)S(1)}, bf16[1,135,64]{2,1,0:T(8,128)(2,1)S(1)}, u32[]{:S(2)}, u32[]{:S(2)}) collective-permute-start(bf16[1,135,64]{2,1,0:T(8,128)(2,1)S(1)} %get-tuple-element.82), channel_id=1, source_target_pairs={{1,0},{2,1},{3,2},{4,3},{5,4},{6,5},{7,6},{8,7},{9,8},{10,9},{11,1... | collective-permute-start | bytes 51848 | tf_op jit(solution)/shard_map/ppermute | solution.py:21
  391.3 8.8 %collective-permute-start.46 = (bf16[1,135,64]{2,1,0:T(8,128)(2,1)S(1)}, bf16[1,135,64]{2,1,0:T(8,128)(2,1)S(1)}, u32[]{:S(2)}, u32[]{:S(2)}) collective-permute-start(bf16[1,135,64]{2,1,0:T(8,128)(2,1)S(1)} %get-tuple-element.80), channel_id=1, source_target_pairs={{1,0},{2,1},{3,2},{4,3},{5,4},{6,5},{7,6},{8,7},{9,8},{10,9},{11,1... | collective-permute-start | bytes 51848 | tf_op jit(solution)/shard_map/ppermute | solution.py:21
  406.9 8.8 %collective-permute-start.48 = (bf16[1,135,64]{2,1,0:T(8,128)(2,1)S(1)}, bf16[1,135,64]{2,1,0:T(8,128)(2,1)S(1)}, u32[]{:S(2)}, u32[]{:S(2)}) collective-permute-start(bf16[1,135,64]{2,1,0:T(8,128)(2,1)S(1)} %get-tuple-element.78), channel_id=1, source_target_pairs={{1,0},{2,1},{3,2},{4,3},{5,4},{6,5},{7,6},{8,7},{9,8},{10,9},{11,1... | collective-permute-start | bytes 51848 | tf_op jit(solution)/shard_map/ppermute | solution.py:21
  429.3 8.8 %collective-permute-start.51 = (bf16[1,135,64]{2,1,0:T(8,128)(2,1)S(1)}, bf16[1,135,64]{2,1,0:T(8,128)(2,1)S(1)}, u32[]{:S(2)}, u32[]{:S(2)}) collective-permute-start(bf16[1,135,64]{2,1,0:T(8,128)(2,1)S(1)} %get-tuple-element.76), channel_id=1, source_target_pairs={{1,0},{2,1},{3,2},{4,3},{5,4},{6,5},{7,6},{8,7},{9,8},{10,9},{11,1... | collective-permute-start | bytes 51848 | tf_op jit(solution)/shard_map/ppermute | solution.py:21
  444.8 8.8 %collective-permute-start.53 = (bf16[1,135,64]{2,1,0:T(8,128)(2,1)S(1)}, bf16[1,135,64]{2,1,0:T(8,128)(2,1)S(1)}, u32[]{:S(2)}, u32[]{:S(2)}) collective-permute-start(bf16[1,135,64]{2,1,0:T(8,128)(2,1)S(1)} %get-tuple-element.74), channel_id=1, source_target_pairs={{1,0},{2,1},{3,2},{4,3},{5,4},{6,5},{7,6},{8,7},{9,8},{10,9},{11,1... | collective-permute-start | bytes 51848 | tf_op jit(solution)/shard_map/ppermute | solution.py:21
  460.4 8.8 %collective-permute-start.55 = (bf16[1,135,64]{2,1,0:T(8,128)(2,1)S(1)}, bf16[1,135,64]{2,1,0:T(8,128)(2,1)S(1)}, u32[]{:S(2)}, u32[]{:S(2)}) collective-permute-start(bf16[1,135,64]{2,1,0:T(8,128)(2,1)S(1)} %get-tuple-element.72), channel_id=1, source_target_pairs={{1,0},{2,1},{3,2},{4,3},{5,4},{6,5},{7,6},{8,7},{9,8},{10,9},{11,1... | collective-permute-start | bytes 51848 | tf_op jit(solution)/shard_map/ppermute | solution.py:21
  475.9 8.8 %collective-permute-start.57 = (bf16[1,135,64]{2,1,0:T(8,128)(2,1)S(1)}, bf16[1,135,64]{2,1,0:T(8,128)(2,1)S(1)}, u32[]{:S(2)}, u32[]{:S(2)}) collective-permute-start(bf16[1,135,64]{2,1,0:T(8,128)(2,1)S(1)} %get-tuple-element.70), channel_id=1, source_target_pairs={{1,0},{2,1},{3,2},{4,3},{5,4},{6,5},{7,6},{8,7},{9,8},{10,9},{11,1... | collective-permute-start | bytes 51848 | tf_op jit(solution)/shard_map/ppermute | solution.py:21
  491.4 8.8 %collective-permute-start.59 = (bf16[1,135,64]{2,1,0:T(8,128)(2,1)S(1)}, bf16[1,135,64]{2,1,0:T(8,128)(2,1)S(1)}, u32[]{:S(2)}, u32[]{:S(2)}) collective-permute-start(bf16[1,135,64]{2,1,0:T(8,128)(2,1)S(1)} %get-tuple-element.68), channel_id=1, source_target_pairs={{1,0},{2,1},{3,2},{4,3},{5,4},{6,5},{7,6},{8,7},{9,8},{10,9},{11,1... | collective-permute-start | bytes 51848 | tf_op jit(solution)/shard_map/ppermute | solution.py:21
  507.0 8.8 %collective-permute-start.61 = (bf16[1,135,64]{2,1,0:T(8,128)(2,1)S(1)}, bf16[1,135,64]{2,1,0:T(8,128)(2,1)S(1)}, u32[]{:S(2)}, u32[]{:S(2)}) collective-permute-start(bf16[1,135,64]{2,1,0:T(8,128)(2,1)S(1)} %get-tuple-element.66), channel_id=1, source_target_pairs={{1,0},{2,1},{3,2},{4,3},{5,4},{6,5},{7,6},{8,7},{9,8},{10,9},{11,1... | collective-permute-start | bytes 51848 | tf_op jit(solution)/shard_map/ppermute | solution.py:21
  522.5 8.8 %collective-permute-start.63 = (bf16[1,135,64]{2,1,0:T(8,128)(2,1)S(1)}, bf16[1,135,64]{2,1,0:T(8,128)(2,1)S(1)}, u32[]{:S(2)}, u32[]{:S(2)}) collective-permute-start(bf16[1,135,64]{2,1,0:T(8,128)(2,1)S(1)} %get-tuple-element.64), channel_id=1, source_target_pairs={{1,0},{2,1},{3,2},{4,3},{5,4},{6,5},{7,6},{8,7},{9,8},{10,9},{11,1... | collective-permute-start | bytes 51848 | tf_op jit(solution)/shard_map/ppermute | solution.py:21
  538.0 8.8 %collective-permute-start.65 = (bf16[1,135,64]{2,1,0:T(8,128)(2,1)S(1)}, bf16[1,135,64]{2,1,0:T(8,128)(2,1)S(1)}, u32[]{:S(2)}, u32[]{:S(2)}) collective-permute-start(bf16[1,135,64]{2,1,0:T(8,128)(2,1)S(1)} %get-tuple-element.62), channel_id=1, source_target_pairs={{1,0},{2,1},{3,2},{4,3},{5,4},{6,5},{7,6},{8,7},{9,8},{10,9},{11,1... | collective-permute-start | bytes 51848 | tf_op jit(solution)/shard_map/ppermute | solution.py:21
  560.3 8.8 %collective-permute-start.68 = (bf16[1,135,64]{2,1,0:T(8,128)(2,1)S(1)}, bf16[1,135,64]{2,1,0:T(8,128)(2,1)S(1)}, u32[]{:S(2)}, u32[]{:S(2)}) collective-permute-start(bf16[1,135,64]{2,1,0:T(8,128)(2,1)S(1)} %get-tuple-element.60), channel_id=1, source_target_pairs={{1,0},{2,1},{3,2},{4,3},{5,4},{6,5},{7,6},{8,7},{9,8},{10,9},{11,1... | collective-permute-start | bytes 51848 | tf_op jit(solution)/shard_map/ppermute | solution.py:21
  575.9 8.8 %collective-permute-start.70 = (bf16[1,135,64]{2,1,0:T(8,128)(2,1)S(1)}, bf16[1,135,64]{2,1,0:T(8,128)(2,1)S(1)}, u32[]{:S(2)}, u32[]{:S(2)}) collective-permute-start(bf16[1,135,64]{2,1,0:T(8,128)(2,1)S(1)} %get-tuple-element.58), channel_id=1, source_target_pairs={{1,0},{2,1},{3,2},{4,3},{5,4},{6,5},{7,6},{8,7},{9,8},{10,9},{11,1... | collective-permute-start | bytes 51848 | tf_op jit(solution)/shard_map/ppermute | solution.py:21
  591.4 8.8 %collective-permute-start.72 = (bf16[1,135,64]{2,1,0:T(8,128)(2,1)S(1)}, bf16[1,135,64]{2,1,0:T(8,128)(2,1)S(1)}, u32[]{:S(2)}, u32[]{:S(2)}) collective-permute-start(bf16[1,135,64]{2,1,0:T(8,128)(2,1)S(1)} %get-tuple-element.56), channel_id=1, source_target_pairs={{1,0},{2,1},{3,2},{4,3},{5,4},{6,5},{7,6},{8,7},{9,8},{10,9},{11,1... | collective-permute-start | bytes 51848 | tf_op jit(solution)/shard_map/ppermute | solution.py:21
  622.5 8.8 %collective-permute-start.76 = (bf16[1,135,64]{2,1,0:T(8,128)(2,1)S(1)}, bf16[1,135,64]{2,1,0:T(8,128)(2,1)S(1)}, u32[]{:S(2)}, u32[]{:S(2)}) collective-permute-start(bf16[1,135,64]{2,1,0:T(8,128)(2,1)S(1)} %get-tuple-element.52), channel_id=1, source_target_pairs={{1,0},{2,1},{3,2},{4,3},{5,4},{6,5},{7,6},{8,7},{9,8},{10,9},{11,1... | collective-permute-start | bytes 51848 | tf_op jit(solution)/shard_map/ppermute | solution.py:21
  685.6 10.0 %collective-permute-start.80 = (bf16[4,135,64]{2,1,0:T(8,128)(2,1)S(1)}, bf16[4,135,64]{2,1,0:T(8,128)(2,1)S(1)}, u32[]{:S(2)}, u32[]{:S(2)}) collective-permute-start(bf16[4,135,64]{2,1,0:T(8,128)(2,1)S(1)} %get-tuple-element.20), channel_id=1, source_target_pairs={{1,0},{2,1},{3,2},{4,3},{5,4},{6,5},{7,6},{8,7},{9,8},{10,9},{11,1... | collective-permute-start | bytes 207368 | tf_op jit(solution)/shard_map/ppermute | solution.py:21
  707.2 10.1 %collective-permute-start.82 = (bf16[4,135,64]{2,1,0:T(8,128)(2,1)S(1)}, bf16[4,135,64]{2,1,0:T(8,128)(2,1)S(1)}, u32[]{:S(2)}, u32[]{:S(2)}) collective-permute-start(bf16[4,135,64]{2,1,0:T(8,128)(2,1)S(1)} %get-tuple-element.18), channel_id=1, source_target_pairs={{1,0},{2,1},{3,2},{4,3},{5,4},{6,5},{7,6},{8,7},{9,8},{10,9},{11,1... | collective-permute-start | bytes 207368 | tf_op jit(solution)/shard_map/ppermute | solution.py:21
  728.7 10.1 %collective-permute-start.84 = (bf16[4,135,64]{2,1,0:T(8,128)(2,1)S(1)}, bf16[4,135,64]{2,1,0:T(8,128)(2,1)S(1)}, u32[]{:S(2)}, u32[]{:S(2)}) collective-permute-start(bf16[4,135,64]{2,1,0:T(8,128)(2,1)S(1)} %get-tuple-element.16), channel_id=1, source_target_pairs={{1,0},{2,1},{3,2},{4,3},{5,4},{6,5},{7,6},{8,7},{9,8},{10,9},{11,1... | collective-permute-start | bytes 207368 | tf_op jit(solution)/shard_map/ppermute | solution.py:21
  750.1 10.2 %collective-permute-start.86 = (bf16[4,135,64]{2,1,0:T(8,128)(2,1)S(1)}, bf16[4,135,64]{2,1,0:T(8,128)(2,1)S(1)}, u32[]{:S(2)}, u32[]{:S(2)}) collective-permute-start(bf16[4,135,64]{2,1,0:T(8,128)(2,1)S(1)} %get-tuple-element.14), channel_id=1, source_target_pairs={{1,0},{2,1},{3,2},{4,3},{5,4},{6,5},{7,6},{8,7},{9,8},{10,9},{11,1... | collective-permute-start | bytes 207368 | tf_op jit(solution)/shard_map/ppermute | solution.py:21
  771.7 10.0 %collective-permute-start.88 = (bf16[4,135,64]{2,1,0:T(8,128)(2,1)S(1)}, bf16[4,135,64]{2,1,0:T(8,128)(2,1)S(1)}, u32[]{:S(2)}, u32[]{:S(2)}) collective-permute-start(bf16[4,135,64]{2,1,0:T(8,128)(2,1)S(1)} %get-tuple-element.12), channel_id=1, source_target_pairs={{1,0},{2,1},{3,2},{4,3},{5,4},{6,5},{7,6},{8,7},{9,8},{10,9},{11,1... | collective-permute-start | bytes 207368 | tf_op jit(solution)/shard_map/ppermute | solution.py:21
  793.1 10.0 %collective-permute-start.90 = (bf16[4,135,64]{2,1,0:T(8,128)(2,1)S(1)}, bf16[4,135,64]{2,1,0:T(8,128)(2,1)S(1)}, u32[]{:S(2)}, u32[]{:S(2)}) collective-permute-start(bf16[4,135,64]{2,1,0:T(8,128)(2,1)S(1)} %get-tuple-element.8), channel_id=1, source_target_pairs={{1,0},{2,1},{3,2},{4,3},{5,4},{6,5},{7,6},{8,7},{9,8},{10,9},{11,1... | collective-permute-start | bytes 207368 | tf_op jit(solution)/shard_map/ppermute | solution.py:21
  (70 other events, 518.0 us)
where the time goes:
time: 824 us; the launch traced here: 813 us
  starting transfers between devices  286 us (35%)
  local copies, waits for them, and re-layouts  232 us (28%)
  waiting for transfers between devices  228 us (28%)
  matrix products  39 us (5%)
  other arithmetic  23.2 us (3%)
    ppermute x46, waiting for transfers between devices, padded(): lax.ppermute(head, axis, [((i + 1) % count, i) for i in range(ends)])  202 us
    ppermute x46, starting transfers between devices, padded(): lax.ppermute(head, axis, [((i + 1) % count, i) for i in range(ends)])  172 us
    gather x60, local copies, waits for them, and re-layouts, neighbours(): gathered = jnp.take(extended, conn_flat, axis=2) * face_keep  158 us
    ppermute x46, starting transfers between devices, padded(): lax.ppermute(tail, axis, [(i, (i + 1) % count) for i in range(ends)])  108 us
    gather x91, local copies, waits for them, and re-layouts, neighbours(): outgoing = jnp.take(iterate, send_index, axis=2)  45.3 us
    dot_general x46, matrix products, propagate(): jnp.einsum('bij,njbk->nibk', chosen, blocked, preferred_element_type=jnp....  39 us
  transfers between devices with their start and end apart: 95, of which 56 were waited for; matrix products, arithmetic and copies ran while one was open for 4% of the time, Pallas kernels for 0%

commit v1 on v0

v1 whole, which is shorter than its diff:
```python
import functools

import jax
import jax.numpy as jnp
from jax import lax
from jax.experimental import pallas as pl
from jax.experimental.pallas import tpu as pltpu
from jax.sharding import PartitionSpec as P

PRISM = 90
COARSEN = 4
LANES = 128
HALF = 64
ROWS = 144
FACES = 6
DEPTH = (FACES + 1) * ROWS
CHAIN = 4
OFFSETS = (1, -1, 2, -2)
MESH = pl.DeviceIdType.MESH
BF = jnp.bfloat16
F32 = jnp.float32


def matmul(left, right):
    return jnp.dot(left, right, preferred_element_type=F32)


def exact(left, right):
    return jnp.dot(left, right, preferred_element_type=F32, precision=lax.Precision.HIGHEST)


def kernel(
    spaces,
    windows,
    initial,
    forcing,
    meta,
    inverses,
    faces,
    out,
    source,
    received,
    gather_one,
    gather_two,
    pick,
    mats,
    own_mats,
    stacked,
    decay,
    drive,
    drive_sel,
    drive_left,
    drive_right,
    residual,
    meta_left,
    meta_right,
    send_sem,
    recv_sem,
    pass_send,
    pass_recv,
    meta_send,
    meta_recv,
    drive_send,
    drive_recv,
):
    place = lax.axis_index("space")
    window = lax.axis_index("tm")
    width = initial.shape[0]

    def inside(shift):
        return jnp.logical_and(place + shift >= 0, place + shift < spaces)

    source[0, 0:CHAIN] = jnp.zeros((CHAIN,) + source.shape[2:], BF)
    received[...] = jnp.zeros(received.shape, BF)
    drive_left[...] = jnp.zeros(drive_left.shape, BF)
    drive_right[...] = jnp.zeros(drive_right.shape, BF)
    meta_left[...] = jnp.zeros(meta_left.shape, F32)
    meta_right[...] = jnp.zeros(meta_right.shape, F32)

    barrier = pltpu.get_barrier_semaphore()
    for shift in OFFSETS:
        @pl.when(inside(shift))
        def _():
            pl.semaphore_signal(
                barrier,
                inc=1,
                device_id={"tm": window, "space": place + shift},
                device_id_type=MESH,
            )
    for shift in (0,) + OFFSETS:
        @pl.when(jnp.logical_and(inside(shift), window > 0))
        def _():
            pl.semaphore_signal(
                barrier,
                inc=1,
                device_id={"tm": window - 1, "space": place + shift},
                device_id_type=MESH,
            )
    beside_count = sum(jnp.where(inside(shift), 1, 0) for shift in OFFSETS)
    pl.semaphore_wait(
        barrier, beside_count + jnp.where(window < windows - 1, beside_count + 1, 0)
    )

    def meta_copy(side):
        shift = (1, -1)[side]
        return pltpu.make_async_remote_copy(
            src_ref=meta,
            dst_ref=(meta_left, meta_right)[side],
            send_sem=meta_send.at[side],
            recv_sem=meta_recv.at[side],
            device_id={"tm": window, "space": place + shift},
            device_id_type=MESH,
        )

    for side in range(2):
        @pl.when(inside((1, -1)[side]))
        def _():
            meta_copy(side).start()

    lane = lax.broadcasted_iota(jnp.int32, (1, LANES), 1)
    low = lane < HALF
    row_of = lax.broadcasted_iota(jnp.int32, (LANES, LANES), 0)
    send_own = meta[0:1, :].astype(jnp.int32)
    kind_own = meta[2:3, :]
    pick_own = (row_of == send_own).astype(F32)
    pick[...] = pick_own.astype(BF)

    drive[...] = jnp.zeros(drive.shape, BF)
    drive_sel[...] = jnp.zeros(drive_sel.shape, BF)

    def fill(index, carry):
        step, item = index // 4, index % 4
        drive[step, item, 0:width, :] = forcing[item * COARSEN + step]
        drive_sel[step, item] = matmul(drive[step, item], pick[...]).astype(BF)
        return carry

    lax.fori_loop(0, 16, fill, 0)

    def drive_copy(step, side):
        shift = (1, -1)[side]
        return pltpu.make_async_remote_copy(
            src_ref=drive_sel.at[step],
            dst_ref=(drive_left, drive_right)[side].at[step],
            send_sem=drive_send.at[step, side],
            recv_sem=drive_recv.at[step, side],
            device_id={"tm": window, "space": place + shift},
            device_id_type=MESH,
        )

    def state_copy(parity, slot, direction, target):
        return pltpu.make_async_remote_copy(
            src_ref=source.at[parity, slot, direction // 2],
            dst_ref=received.at[parity, slot, direction],
            send_sem=send_sem.at[parity, slot, direction],
            recv_sem=recv_sem.at[parity, slot, direction],
            device_id={"tm": target, "space": place + OFFSETS[direction]},
            device_id_type=MESH,
        )

    def pass_copy(part, target):
        return pltpu.make_async_remote_copy(
            src_ref=source.at[0, CHAIN, part],
            dst_ref=source.at[0, CHAIN, part],
            send_sem=pass_send.at[part],
            recv_sem=pass_recv.at[part],
            device_id={"tm": target, "space": place},
            device_id_type=MESH,
        )

    def send_state(parity, slot, target):
        for direction in range(4):
            @pl.when(inside(OFFSETS[direction]))
            def _():
                state_copy(parity, slot, direction, target).start()

    def await_state(parity, slot):
        for direction in range(4):
            @pl.when(inside(-OFFSETS[direction]))
            def _():
                state_copy(parity, slot, direction, window).wait_recv()

    def await_sent(parity, slot):
        for direction in range(4):
            @pl.when(inside(OFFSETS[direction]))
            def _():
                state_copy(parity, slot, direction, window).wait_send()

    for step in range(4):
        for side in range(2):
            @pl.when(inside((1, -1)[side]))
            def _():
                drive_copy(step, side).start()

    tall = lax.broadcasted_iota(jnp.int32, (width, LANES), 0)
    kept = jnp.logical_and(
        jnp.logical_or(tall < PRISM, kind_own < 0.5), jnp.broadcast_to(window, (1, 1)) == 0
    )
    source[0, 0, 0, 0:width, :] = jnp.where(kept, initial[...], jnp.zeros_like(initial))
    source[0, 0, 1] = matmul(source[0, 0, 0], pick[...]).astype(BF)

    @pl.when(window == 0)
    def _():
        send_state(0, 0, window)

    for index in range(4):
        mats[index] = matmul(inverses[index], faces[...]).astype(BF)
    for step in range(2):
        own_mats[step] = jnp.where(
            jnp.broadcast_to(meta[2:3, 0:1], (1, 1)) < 0.5, mats[2 * step], mats[2 * step + 1]
        )

    for side in range(2):
        @pl.when(inside((-1, 1)[side]))
        def _():
            meta_copy(side).wait_recv()
    for side in range(2):
        @pl.when(inside((1, -1)[side]))
        def _():
            meta_copy(side).wait_send()

    send_left = meta_left[0:1, :].astype(jnp.int32)
    send_right = meta_right[0:1, :].astype(jnp.int32)
    listed_left = exact(meta_left[...], (row_of == send_left).astype(F32))
    listed_right = exact(meta_right[...], (row_of == send_right).astype(F32))
    listed_own = exact(meta[...], pick_own)
    beside = jnp.where(low, listed_right, listed_left)
    there = jnp.where(
        low,
        jnp.broadcast_to(inside(1).astype(jnp.int32), (1, LANES)),
        jnp.broadcast_to(inside(-1).astype(jnp.int32), (1, LANES)),
    )
    for step in range(2):
        scale = -1.0 if step == 0 else -1.0 * COARSEN
        decay[step, 0:1, :] = jnp.exp(scale * meta[1:2, :])
        decay[step, 1:2, :] = jnp.exp(scale * beside[1:2, :]) * there.astype(F32)
        decay[step, 2:3, :] = jnp.exp(scale * listed_own[1:2, :])
    decay[0, 3:4, :] = kind_own
    decay[0, 4:5, :] = beside[2:3, :]

    def turned(row):
        return jnp.concatenate([row[:, HALF:], row[:, :HALF]], axis=1)

    own_map = jnp.concatenate(
        [LANES + lane, jnp.where(low, turned(send_left), 2 * LANES + turned(send_right))], axis=1
    )
    left_map = jnp.concatenate(
        [lane, jnp.where(low, 3 * LANES + HALF + lane, LANES + turned(send_own))], axis=1
    )
    right_map = jnp.concatenate(
        [2 * LANES + lane, jnp.where(low, LANES + turned(send_own), 3 * LANES + lane - HALF)], axis=1
    )
    filler = jnp.zeros((5, 2 * LANES), jnp.int32)
    maps = jnp.concatenate([own_map, left_map, right_map, filler], axis=0).astype(F32)
    code = lax.broadcasted_iota(jnp.int32, (2 * LANES, LANES), 0)
    spot = lax.broadcasted_iota(jnp.int32, (4 * LANES, LANES), 0)

    def whole(row):
        return (row + 0.5).astype(jnp.int32)

    def second(row):
        return jnp.where(row < LANES, row, jnp.where(row < LANES + HALF, row + HALF, row - HALF))

    for face in range(FACES):
        conn_own = whole(meta[8 + face : 9 + face, :])
        conn_beside = whole(beside[8 + face : 9 + face, :])
        conn_listed = whole(listed_own[8 + face : 9 + face, :])
        at_own = whole(exact(maps, (code == conn_own).astype(F32))[0:1, :])
        both = whole(exact(maps, (code == conn_beside).astype(F32)))
        at_beside = jnp.where(low, both[2:3, :], both[1:2, :])
        at_beside = jnp.where(there > 0, at_beside, -1)
        two_own = second(conn_own)
        two_listed = second(conn_listed)
        if face == FACES - 1:
            at_own = jnp.where(kind_own < 0.5, at_own, -1)
            two_own = jnp.where(kind_own < 0.5, two_own, -1)
            two_listed = jnp.where(kind_own < 0.5, two_listed, -1)
            at_beside = jnp.where(beside[2:3, :] < 0.5, at_beside, -1)
        here = slice(face * LANES, (face + 1) * LANES)
        after = slice((FACES + face) * LANES, (FACES + face + 1) * LANES)
        gather_one[:, here] = (spot == at_own).astype(F32).astype(BF)
        gather_one[:, after] = (spot == at_beside).astype(F32).astype(BF)
        gather_two[:, here] = (code == two_own).astype(F32).astype(BF)
        gather_two[:, after] = (code == two_listed).astype(F32).astype(BF)
    at_listed = jnp.where(low, 2 * LANES + send_right, send_left)
    at_listed = jnp.where(there > 0, at_listed, -1)
    gather_one[:, 2 * FACES * LANES :] = (spot == at_listed).astype(F32).astype(BF)

    residual[CHAIN] = jnp.zeros((ROWS, 2 * LANES), BF)

    def job(turn, item):
        early = turn < 4
        middle = jnp.logical_and(turn >= 4, turn < 8)
        coarse = jnp.logical_and(middle, item == 0)
        first = window == 0
        parity = jnp.where(middle, 0, turn % 2)
        slot = jnp.where(middle, turn, item)
        op = jnp.where(coarse, 1, 0)

        fresh = jnp.where(
            early,
            jnp.logical_or(turn >= 1, jnp.logical_and(item == 0, first)),
            jnp.logical_not(jnp.logical_and(middle, item == 1)),
        )
        handed = jnp.logical_and(turn == 4, item == 0)

        @pl.when(fresh)
        def _():
            await_state(parity, slot)

        @pl.when(jnp.logical_and(fresh, jnp.logical_not(handed)))
        def _():
            await_sent(parity, slot)

        @pl.when(handed)
        def _():
            for part in range(2):
                pass_copy(part, window).wait_recv()

        @pl.when(jnp.logical_and(early, item == 0))
        def _():
            for side in range(2):
                @pl.when(inside((-1, 1)[side]))
                def _():
                    drive_copy(turn, side).wait_recv()
            for side in range(2):
                @pl.when(inside((1, -1)[side]))
                def _():
                    drive_copy(turn, side).wait_send()

        fine_step = jnp.where(early, turn, jnp.where(middle, 0, turn - 7))
        fine_item = jnp.where(middle, turn - 4, item)
        drive_step = jnp.where(coarse, 4, fine_step)
        drive_item = jnp.where(coarse, 0, fine_item)
        drive_at = jnp.where(coarse, 0.0, 1.0)

        own = source[parity, slot, 0]
        listed = source[parity, slot, 1]
        outer = jnp.where(low, received[parity, slot, 3], received[parity, slot, 2])
        near = jnp.concatenate([received[parity, slot, 0], own], axis=1)
        far = jnp.concatenate([received[parity, slot, 1], outer], axis=1)
        decay_now = decay[op]
        drive_beside = jnp.where(
            low, drive_right[fine_step, fine_item], drive_left[fine_step, fine_item]
        )
        rhs_own = decay_now[0:1, :] * own.astype(F32) + drive_at * drive[
            fine_step, fine_item
        ].astype(F32)
        rhs_listed = decay_now[2:3, :] * listed.astype(F32) + drive_at * drive_sel[
            fine_step, fine_item
        ].astype(F32)

        def stack(gathered):
            gathered = gathered.astype(BF)
            for face in range(FACES):
                rows = slice(face * ROWS, (face + 1) * ROWS)
                stacked[rows, 0:LANES] = gathered[:, face * LANES : (face + 1) * LANES]
                stacked[rows, LANES : 2 * LANES] = gathered[
                    :, (FACES + face) * LANES : (FACES + face + 1) * LANES
                ]

        tail = slice(FACES * ROWS, DEPTH)
        gathered = matmul(near, gather_one[0 : 2 * LANES, :]) + matmul(
            far, gather_one[2 * LANES :, :]
        )
        stack(gathered)
        stacked[tail, 0:LANES] = rhs_own.astype(BF)
        rhs_beside = decay_now[1:2, :] * gathered[
            :, 2 * FACES * LANES :
        ] + drive_at * drive_beside.astype(F32)
        stacked[tail, LANES : 2 * LANES] = rhs_beside.astype(BF)
        kinds = jnp.concatenate([decay[0, 3:4, :], decay[0, 4:5, :]], axis=1)
        once = jnp.where(
            kinds < 0.5,
            matmul(mats[2 * op], stacked[...]),
            matmul(mats[2 * op + 1], stacked[...]),
        ).astype(BF)

        stack(matmul(once, gather_two[...]))
        stacked[tail, LANES : 2 * LANES] = rhs_listed.astype(BF)
        plus = residual[jnp.where(coarse, turn - 4, CHAIN)].astype(F32)
        twice = (matmul(own_mats[op], stacked[...]) + plus).astype(BF)

        leading = jnp.logical_and(first, item == 0)
        last_early = turn == 3

        @pl.when(last_early)
        def _():
            residual[item] = twice

        sending = jnp.where(
            early,
            jnp.logical_or(turn < 3, leading),
            jnp.where(
                coarse,
                jnp.logical_or(turn < 7, window < windows - 1),
                turn < 9,
            ),
        )
        fine = jnp.logical_and(middle, item == 1)
        out_slot = jnp.where(
            early,
            jnp.where(last_early, CHAIN + 1, item),
            jnp.where(
                coarse,
                jnp.where(turn == 7, CHAIN, turn + 1),
                jnp.where(fine, turn - 4, item),
            ),
        )
        out_parity = jnp.where(jnp.logical_or(middle, last_early), 0, (turn + 1) % 2)
        leaving = jnp.logical_and(coarse, turn == 7)
        target = jnp.where(leaving, window + 1, window)

        @pl.when(sending)
        def _():
            source[out_parity, out_slot, 0] = twice[:, 0:LANES]
            source[out_parity, out_slot, 1] = twice[:, LANES:]
            send_state(out_parity, out_slot, target)

            @pl.when(leaving)
            def _():
                for part in range(2):
                    pass_copy(part, target).start()

        out_index = jnp.where(
            early,
            turn,
            jnp.where(
                coarse,
                COARSEN * (turn - 4) + COARSEN - 1,
                jnp.where(fine, COARSEN * (turn - 4), COARSEN * item + turn - 7),
            ),
        )

        @pl.when(jnp.logical_or(jnp.logical_not(early), leading))
        def _():
            out[out_index] = twice[0:width, 0:LANES]

    def round_of(turn, carry):
        early = turn < 4
        middle = jnp.logical_and(turn >= 4, turn < 8)
        begin = jnp.where(jnp.logical_and(turn >= 8, window == 0), 1, 0)
        jobs = jnp.where(
            middle, jnp.where(jnp.logical_and(turn == 4, window == 0), 0, 2), 4
        )

        def one(item, inner):
            job(turn, item)
            return inner

        lax.fori_loop(begin, jobs, one, 0)
        return carry

    lax.fori_loop(0, 10, round_of, 0)

    @pl.when(window < windows - 1)
    def _():
        await_sent(0, CHAIN)
        for part in range(2):
            pass_copy(part, window + 1).wait_send()


def shards(initial, forcing, damping, block_inv, coarse_inv, coupling, etype, send_index, conn):
    width = initial.shape[0]
    steps = forcing.shape[0]
    spaces = lax.axis_size("space")
    windows = lax.axis_size("tm")
    grow = ROWS - width
    inverses = jnp.pad(
        jnp.concatenate([block_inv, coarse_inv], axis=0), ((0, 0), (0, grow), (0, grow))
    )
    unit = jnp.eye(ROWS, dtype=BF)[None]
    faces = jnp.concatenate([jnp.pad(-coupling, ((0, 0), (0, grow), (0, grow))), unit], axis=0)
    faces = faces.transpose(1, 0, 2).reshape(ROWS, DEPTH)
    meta = jnp.concatenate(
        [
            send_index.astype(F32)[None],
            damping[None],
            jnp.broadcast_to(etype.astype(F32)[:, None], (1, LANES)),
            jnp.zeros((5, LANES), F32),
            conn.astype(F32),
            jnp.zeros((2, LANES), F32),
        ],
        axis=0,
    )
    vmem = pl.BlockSpec(memory_space=pltpu.VMEM)
    dma = pltpu.SemaphoreType.DMA
    return pl.pallas_call(
        functools.partial(kernel, spaces, windows),
        out_shape=jax.ShapeDtypeStruct((steps, width, LANES), BF),
        in_specs=[vmem] * 5,
        out_specs=vmem,
        scratch_shapes=[
            pltpu.VMEM((2, 8, 2, ROWS, LANES), BF),
            pltpu.VMEM((2, 8, 4, ROWS, LANES), BF),
            pltpu.VMEM((4 * LANES, 13 * LANES), BF),
            pltpu.VMEM((2 * LANES, 12 * LANES), BF),
            pltpu.VMEM((LANES, LANES), BF),
            pltpu.VMEM((4, ROWS, DEPTH), BF),
            pltpu.VMEM((2, ROWS, DEPTH), BF),
            pltpu.VMEM((DEPTH, 2 * LANES), BF),
            pltpu.VMEM((2, 8, LANES), F32),
            pltpu.VMEM((4, 4, ROWS, LANES), BF),
            pltpu.VMEM((4, 4, ROWS, LANES), BF),
            pltpu.VMEM((4, 4, ROWS, LANES), BF),
            pltpu.VMEM((4, 4, ROWS, LANES), BF),
            pltpu.VMEM((5, ROWS, 2 * LANES), BF),
            pltpu.VMEM((16, LANES), F32),
            pltpu.VMEM((16, LANES), F32),
            dma((2, 8, 4)),
            dma((2, 8, 4)),
            dma((2,)),
            dma((2,)),
            dma((2,)),
            dma((2,)),
            dma((4, 2)),
            dma((4, 2)),
        ],
        compiler_params=pltpu.CompilerParams(
            collective_id=0, has_side_effects=True, vmem_limit_bytes=48 << 20
        ),
    )(initial, forcing, meta, inverses, faces)


def solution(mesh):
    in_specs = (
        P(None, "space"),
        P("tm", None, "space"),
        P("space"),
        P(),
        P(),
        P(),
        P("space"),
        P("space"),
        P(None, "space"),
    )
    out_specs = P("tm", None, "space")
    return jax.shard_map(shards, mesh=mesh, in_specs=in_specs, out_specs=out_specs, check_vma=False)
```

time: 824 us -> 158 us (0.19)
  the two profiles are of different devices: /device:TPU:122 before, /device:TPU:71 now
where the time goes in v1:
time: 158 us
  Pallas kernels  151 us (96%)
  local copies, waits for them, and re-layouts  6.08 us (4%)
    pallas_call x1, Pallas kernels, shards(): pl.pallas_call(functools.partial(kernel, spaces, windows), out_shape=jax....  151 us
    unnamed x17, local copies, waits for them, and re-layouts  4.5 us

profile of v1, /device:TPU:71, one launch (start us, length us, event | category | flops | bytes accessed | tf_op | source)
XLA Modules:
  0.0 158.0 jit_solution(17171819908876154808)
XLA Ops:
  0.7 0.0 copy-start.4
  0.7 0.0 copy-start.6
  0.7 0.6 copy-done.6
  1.3 0.0 copy-done.4
  1.3 0.0 copy-start.5
  1.4 0.6 copy-done.5
  2.1 0.0 copy-start.3
  2.1 1.0 copy.15
  3.0 0.0 copy-done.3
  3.1 0.0 copy-start.2
  3.1 0.1 fusion.8.inverses
  3.2 0.9 copy-done.2
  4.1 0.1 neg.3
  4.1 0.1 fusion.5
  4.2 0.2 copy.17
  4.4 0.0 copy-start.1
  4.4 0.5 reshape.20.faces
  4.9 0.6 copy-done.1
  5.5 0.0 copy-start
  5.5 0.1 copy.18.forcing
  5.6 0.6 copy-done
  6.2 150.8 %shard_map.91 = bf16[16,135,128]{2,1,0:T(8,128)(2,1)S(1)} custom-call(bf16[135,128]{1,0:T(8,128)(2,1)S(1)} %copy-done, bf16[16,135,128]{2,1,0:T(8,128)(2,1)S(1)} %copy.18.forcing, f32[16,128]{1,0:T(8,128)S(1)} %concatenate.9.meta, bf16[4,144,144]{2,1,0:T(8,128)(2,1)S(1)} %fusion.8.inverses, bf16[144,1008]{1,0:T(8,128)(2,1)S(1)} %reshape.20.faces), custom_call_target="tpu_custom_call" | custom-call | tf_op jit(solution)/shard_map/pallas_call | solution.py:487
  157.1 0.9 copy.19
  (8 shorter events, 0.1 us)
Async XLA Ops:
  0.7 0.7 copy-start.4
  0.7 0.7 copy-start.6
  1.3 0.7 copy-start.5
  2.1 1.0 copy-start.3
  3.1 1.0 copy-start.2
  4.4 1.1 copy-start.1
  5.5 0.8 copy-start

commit v2 on v1

--- a/solution.py
+++ b/solution.py
@@ -15,6 +15,7 @@
 FACES = 6
 DEPTH = (FACES + 1) * ROWS
 CHAIN = 4
+GATED = 1
 OFFSETS = (1, -1, 2, -2)
 MESH = pl.DeviceIdType.MESH
 BF = jnp.bfloat16
@@ -25,19 +26,30 @@
     return jnp.dot(left, right, preferred_element_type=F32)
 
 
-def exact(left, right):
-    return jnp.dot(left, right, preferred_element_type=F32, precision=lax.Precision.HIGHEST)
+def take(table, index):
+    return jnp.take_along_axis(table, index, axis=1, mode="promise_in_bounds")
 
 
 def kernel(
     spaces,
     windows,
+    initial_in,
+    forcing_in,
+    damping,
+    block_in,
+    coarse_in,
+    coupling_in,
+    etype,
+    send_index,
+    conn,
+    out,
     initial,
     forcing,
+    inverse,
+    coupling,
+    padded,
+    faces,
     meta,
-    inverses,
-    faces,
-    out,
     source,
     received,
     gather_one,
@@ -49,11 +61,13 @@
     decay,
     drive,
     drive_sel,
+    drive_out,
     drive_left,
     drive_right,
     residual,
     meta_left,
     meta_right,
+    load_sem,
     send_sem,
     recv_sem,
     pass_send,
@@ -62,6 +76,7 @@
     meta_recv,
     drive_send,
     drive_recv,
+    gate,
 ):
     place = lax.axis_index("space")
     window = lax.axis_index("tm")
@@ -70,12 +85,26 @@
     def inside(shift):
         return jnp.logical_and(place + shift >= 0, place + shift < spaces)
 
-    source[0, 0:CHAIN] = jnp.zeros((CHAIN,) + source.shape[2:], BF)
-    received[...] = jnp.zeros(received.shape, BF)
-    drive_left[...] = jnp.zeros(drive_left.shape, BF)
-    drive_right[...] = jnp.zeros(drive_right.shape, BF)
-    meta_left[...] = jnp.zeros(meta_left.shape, F32)
-    meta_right[...] = jnp.zeros(meta_right.shape, F32)
+    loads = [
+        pltpu.make_async_copy(initial_in, initial, load_sem.at[0]),
+        pltpu.make_async_copy(forcing_in, forcing, load_sem.at[1]),
+        pltpu.make_async_copy(block_in, inverse.at[0:2], load_sem.at[2]),
+        pltpu.make_async_copy(coarse_in, inverse.at[2:4], load_sem.at[3]),
+        pltpu.make_async_copy(coupling_in, coupling, load_sem.at[4]),
+    ]
+    for load in loads:
+        load.start()
+
+    received[0, 0:CHAIN] = jnp.zeros((CHAIN,) + received.shape[2:], BF)
+
+    @pl.when(jnp.logical_or(place < 2, place >= spaces - 2))
+    def _():
+        received[0, CHAIN:] = jnp.zeros((CHAIN,) + received.shape[2:], BF)
+        received[1, 0:CHAIN] = jnp.zeros((CHAIN,) + received.shape[2:], BF)
+        drive_left[...] = jnp.zeros(drive_left.shape, BF)
+        drive_right[...] = jnp.zeros(drive_right.shape, BF)
+        meta_left[...] = jnp.zeros(meta_left.shape, F32)
+        meta_right[...] = jnp.zeros(meta_right.shape, F32)
 
     barrier = pltpu.get_barrier_semaphore()
     for shift in OFFSETS:
@@ -96,10 +125,6 @@
                 device_id={"tm": window - 1, "space": place + shift},
                 device_id_type=MESH,
             )
-    beside_count = sum(jnp.where(inside(shift), 1, 0) for shift in OFFSETS)
-    pl.semaphore_wait(
-        barrier, beside_count + jnp.where(window < windows - 1, beside_count + 1, 0)
-    )
 
     def meta_copy(side):
         shift = (1, -1)[side]
@@ -112,34 +137,10 @@
             device_id_type=MESH,
         )
 
-    for side in range(2):
-        @pl.when(inside((1, -1)[side]))
-        def _():
-            meta_copy(side).start()
-
-    lane = lax.broadcasted_iota(jnp.int32, (1, LANES), 1)
-    low = lane < HALF
-    row_of = lax.broadcasted_iota(jnp.int32, (LANES, LANES), 0)
-    send_own = meta[0:1, :].astype(jnp.int32)
-    kind_own = meta[2:3, :]
-    pick_own = (row_of == send_own).astype(F32)
-    pick[...] = pick_own.astype(BF)
-
-    drive[...] = jnp.zeros(drive.shape, BF)
-    drive_sel[...] = jnp.zeros(drive_sel.shape, BF)
-
-    def fill(index, carry):
-        step, item = index // 4, index % 4
-        drive[step, item, 0:width, :] = forcing[item * COARSEN + step]
-        drive_sel[step, item] = matmul(drive[step, item], pick[...]).astype(BF)
-        return carry
-
-    lax.fori_loop(0, 16, fill, 0)
-
     def drive_copy(step, side):
         shift = (1, -1)[side]
         return pltpu.make_async_remote_copy(
-            src_ref=drive_sel.at[step],
+            src_ref=drive_out.at[side, step],
             dst_ref=(drive_left, drive_right)[side].at[step],
             send_sem=drive_send.at[step, side],
             recv_sem=drive_recv.at[step, side],
@@ -185,29 +186,120 @@
             def _():
                 state_copy(parity, slot, direction, window).wait_send()
 
-    for step in range(4):
+    def send_drive(step):
         for side in range(2):
             @pl.when(inside((1, -1)[side]))
             def _():
                 drive_copy(step, side).start()
 
+    def turned(row):
+        return jnp.concatenate([row[:, HALF:], row[:, :HALF]], axis=1)
+
+    def fill(step):
+        def one(item, carry):
+            drive[step, item, 0:width, :] = forcing[item * COARSEN + step]
+            drive_sel[step, item] = matmul(drive[step, item], pick[...]).astype(BF)
+            return carry
+
+        lax.fori_loop(0, CHAIN, one, 0)
+        for pair in range(2):
+            even = drive_sel[step, 2 * pair]
+            odd = turned(drive_sel[step, 2 * pair + 1])
+            drive_out[0, step, pair] = jnp.where(low, odd, even)
+            drive_out[1, step, pair] = jnp.where(low, even, odd)
+
+    lane = lax.broadcasted_iota(jnp.int32, (1, LANES), 1)
+    low = lane < HALF
+    code = lax.broadcasted_iota(jnp.int32, (2 * LANES, LANES), 0)
+    spot = lax.broadcasted_iota(jnp.int32, (4 * LANES, LANES), 0)
+
+    meta[...] = jnp.zeros(meta.shape, F32)
+    meta[0:1, :] = send_index[...].astype(F32)
+    meta[1:2, :] = damping[...]
+    meta[2:3, :] = jnp.broadcast_to(etype[...].astype(F32), (1, LANES))
+    meta[8 : 8 + FACES, :] = conn[...].astype(F32)
+    send_own = send_index[...]
+    kind_own = meta[2:3, :]
+    pick[...] = (code[0:LANES] == send_own).astype(F32).astype(BF)
+
+    source[0, 0:CHAIN] = jnp.zeros((CHAIN,) + source.shape[2:], BF)
     tall = lax.broadcasted_iota(jnp.int32, (width, LANES), 0)
     kept = jnp.logical_and(
         jnp.logical_or(tall < PRISM, kind_own < 0.5), jnp.broadcast_to(window, (1, 1)) == 0
     )
+    loads[0].wait()
     source[0, 0, 0, 0:width, :] = jnp.where(kept, initial[...], jnp.zeros_like(initial))
     source[0, 0, 1] = matmul(source[0, 0, 0], pick[...]).astype(BF)
+    drive[:, :, LANES:, :] = jnp.zeros((CHAIN, CHAIN, ROWS - LANES, LANES), BF)
+    loads[1].wait()
+    fill(0)
+
+    beside_count = sum(jnp.where(inside(shift), 1, 0) for shift in OFFSETS)
+    pl.semaphore_wait(
+        barrier, beside_count + jnp.where(window < windows - 1, beside_count + 1, 0)
+    )
+    for side in range(2):
+        @pl.when(inside((1, -1)[side]))
+        def _():
+            meta_copy(side).start()
 
     @pl.when(window == 0)
     def _():
         send_state(0, 0, window)
 
+    @pl.when(window % 2 == 0)
+    def _():
+        send_drive(0)
+
+    for load in loads[2:]:
+        load.wait()
+    padded[...] = jnp.zeros(padded.shape, BF)
+    padded[0:FACES, 0:width, 0:width] = -coupling[...]
+    padded[FACES:, 0:width, 0:width] = inverse[...]
+    across = lax.broadcasted_iota(jnp.int32, (ROWS, DEPTH), 1)
+    down = lax.broadcasted_iota(jnp.int32, (ROWS, DEPTH), 0)
+    placed = jnp.where(across == down + FACES * ROWS, 1.0, 0.0)
+    for face in range(FACES):
+        shifted = jnp.where(across == down + face * ROWS, 1.0, 0.0).astype(BF)
+        placed = placed + matmul(padded[face], shifted)
+    faces[...] = placed.astype(BF)
     for index in range(4):
-        mats[index] = matmul(inverses[index], faces[...]).astype(BF)
+        mats[index] = matmul(padded[FACES + index], faces[...]).astype(BF)
     for step in range(2):
-        own_mats[step] = jnp.where(
-            jnp.broadcast_to(meta[2:3, 0:1], (1, 1)) < 0.5, mats[2 * step], mats[2 * step + 1]
-        )
+        own_mats[step] = jnp.where(meta[2:3, 0:1] < 0.5, mats[2 * step], mats[2 * step + 1])
+
+    def spread(row):
+        return jnp.broadcast_to(row, (8, LANES))
+
+    def whole(rows):
+        return (rows + 0.5).astype(jnp.int32)
+
+    def onehot(rows, index):
+        return (rows == index).astype(F32).astype(BF)
+
+    def located(codes, start, listed_at):
+        past = jnp.maximum(codes - LANES, 0)
+        return jnp.where(codes < LANES, start + codes, take(spread(listed_at), past))
+
+    def second(codes):
+        return jnp.where(
+            codes < LANES, codes, jnp.where(codes < LANES + HALF, codes + HALF, codes - HALF)
+        )
+
+    last_face = lax.broadcasted_iota(jnp.int32, (8, LANES), 0) == FACES - 1
+
+    def masked(index, kind):
+        return jnp.where(jnp.logical_and(last_face, kind > 0.5), -1, index)
+
+    conn_own = whole(meta[8:16, :])
+    damp_listed = take(meta[0:8, :], spread(send_own))[1:2, :]
+    two_own = masked(second(conn_own), kind_own)
+    two_listed = masked(second(take(conn_own, spread(send_own))), kind_own)
+    for face in range(FACES):
+        here = slice(face * LANES, (face + 1) * LANES)
+        after = slice((FACES + face) * LANES, (FACES + face + 1) * LANES)
+        gather_two[:, here] = onehot(code, two_own[face : face + 1, :])
+        gather_two[:, after] = onehot(code, two_listed[face : face + 1, :])
 
     for side in range(2):
         @pl.when(inside((-1, 1)[side]))
@@ -218,12 +310,14 @@
         def _():
             meta_copy(side).wait_send()
 
-    send_left = meta_left[0:1, :].astype(jnp.int32)
-    send_right = meta_right[0:1, :].astype(jnp.int32)
-    listed_left = exact(meta_left[...], (row_of == send_left).astype(F32))
-    listed_right = exact(meta_right[...], (row_of == send_right).astype(F32))
-    listed_own = exact(meta[...], pick_own)
-    beside = jnp.where(low, listed_right, listed_left)
+    send_left = whole(meta_left[0:1, :])
+    send_right = whole(meta_right[0:1, :])
+    conn_left = whole(take(meta_left[8:16, :], spread(send_left)))
+    conn_right = whole(take(meta_right[8:16, :], spread(send_right)))
+    damp_left = take(meta_left[0:8, :], spread(send_left))[1:2, :]
+    damp_right = take(meta_right[0:8, :], spread(send_right))[1:2, :]
+    damp_beside = jnp.where(low, damp_right, damp_left)
+    kind_beside = jnp.where(low, meta_right[2:3, :], meta_left[2:3, :])
     there = jnp.where(
         low,
         jnp.broadcast_to(inside(1).astype(jnp.int32), (1, LANES)),
@@ -232,65 +326,48 @@
     for step in range(2):
         scale = -1.0 if step == 0 else -1.0 * COARSEN
         decay[step, 0:1, :] = jnp.exp(scale * meta[1:2, :])
-        decay[step, 1:2, :] = jnp.exp(scale * beside[1:2, :]) * there.astype(F32)
-        decay[step, 2:3, :] = jnp.exp(scale * listed_own[1:2, :])
+        decay[step, 1:2, :] = jnp.exp(scale * damp_beside) * there.astype(F32)
+        decay[step, 2:3, :] = jnp.exp(scale * damp_listed)
     decay[0, 3:4, :] = kind_own
-    decay[0, 4:5, :] = beside[2:3, :]
-
-    def turned(row):
-        return jnp.concatenate([row[:, HALF:], row[:, :HALF]], axis=1)
-
-    own_map = jnp.concatenate(
-        [LANES + lane, jnp.where(low, turned(send_left), 2 * LANES + turned(send_right))], axis=1
-    )
-    left_map = jnp.concatenate(
-        [lane, jnp.where(low, 3 * LANES + HALF + lane, LANES + turned(send_own))], axis=1
-    )
-    right_map = jnp.concatenate(
-        [2 * LANES + lane, jnp.where(low, LANES + turned(send_own), 3 * LANES + lane - HALF)], axis=1
-    )
-    filler = jnp.zeros((5, 2 * LANES), jnp.int32)
-    maps = jnp.concatenate([own_map, left_map, right_map, filler], axis=0).astype(F32)
-    code = lax.broadcasted_iota(jnp.int32, (2 * LANES, LANES), 0)
-    spot = lax.broadcasted_iota(jnp.int32, (4 * LANES, LANES), 0)
-
-    def whole(row):
-        return (row + 0.5).astype(jnp.int32)
-
-    def second(row):
-        return jnp.where(row < LANES, row, jnp.where(row < LANES + HALF, row + HALF, row - HALF))
-
+    decay[0, 4:5, :] = kind_beside
+
+    at_own = located(
+        conn_own, LANES, jnp.where(low, turned(send_left), 2 * LANES + turned(send_right))
+    )
+    at_left = located(
+        conn_left, 0, jnp.where(low, 3 * LANES + HALF + lane, LANES + turned(send_own))
+    )
+    at_right = located(
+        conn_right,
+        2 * LANES,
+        jnp.where(low, LANES + turned(send_own), 3 * LANES + lane - HALF),
+    )
+    at_own = masked(at_own, kind_own)
+    at_beside = masked(jnp.where(low, at_right, at_left), kind_beside)
+    at_beside = jnp.where(there > 0, at_beside, -1)
     for face in range(FACES):
-        conn_own = whole(meta[8 + face : 9 + face, :])
-        conn_beside = whole(beside[8 + face : 9 + face, :])
-        conn_listed = whole(listed_own[8 + face : 9 + face, :])
-        at_own = whole(exact(maps, (code == conn_own).astype(F32))[0:1, :])
-        both = whole(exact(maps, (code == conn_beside).astype(F32)))
-        at_beside = jnp.where(low, both[2:3, :], both[1:2, :])
-        at_beside = jnp.where(there > 0, at_beside, -1)
-        two_own = second(conn_own)
-        two_listed = second(conn_listed)
-        if face == FACES - 1:
-            at_own = jnp.where(kind_own < 0.5, at_own, -1)
-            two_own = jnp.where(kind_own < 0.5, two_own, -1)
-            two_listed = jnp.where(kind_own < 0.5, two_listed, -1)
-            at_beside = jnp.where(beside[2:3, :] < 0.5, at_beside, -1)
         here = slice(face * LANES, (face + 1) * LANES)
         after = slice((FACES + face) * LANES, (FACES + face + 1) * LANES)
-        gather_one[:, here] = (spot == at_own).astype(F32).astype(BF)
-        gather_one[:, after] = (spot == at_beside).astype(F32).astype(BF)
-        gather_two[:, here] = (code == two_own).astype(F32).astype(BF)
-        gather_two[:, after] = (code == two_listed).astype(F32).astype(BF)
+        gather_one[:, here] = onehot(spot, at_own[face : face + 1, :])
+        gather_one[:, after] = onehot(spot, at_beside[face : face + 1, :])
     at_listed = jnp.where(low, 2 * LANES + send_right, send_left)
     at_listed = jnp.where(there > 0, at_listed, -1)
-    gather_one[:, 2 * FACES * LANES :] = (spot == at_listed).astype(F32).astype(BF)
+    gather_one[:, 2 * FACES * LANES :] = onehot(spot, at_listed)
 
     residual[CHAIN] = jnp.zeros((ROWS, 2 * LANES), BF)
+
+    @pl.when(window % 2 == 1)
+    def _():
+        pl.semaphore_wait(gate, 1)
+        send_drive(0)
+
 
     def job(turn, item):
         early = turn < 4
         middle = jnp.logical_and(turn >= 4, turn < 8)
-        coarse = jnp.logical_and(middle, item == 0)
+        ending = jnp.logical_and(turn == 7, window == windows - 1)
+        fine = jnp.logical_and(middle, item == jnp.where(ending, 0, 1))
+        coarse = jnp.logical_and(middle, jnp.logical_not(fine))
         first = window == 0
         parity = jnp.where(middle, 0, turn % 2)
         slot = jnp.where(middle, turn, item)
@@ -339,8 +416,12 @@
         near = jnp.concatenate([received[parity, slot, 0], own], axis=1)
         far = jnp.concatenate([received[parity, slot, 1], outer], axis=1)
         decay_now = decay[op]
+        from_left = drive_left[fine_step, fine_item // 2]
+        from_right = drive_right[fine_step, fine_item // 2]
         drive_beside = jnp.where(
-            low, drive_right[fine_step, fine_item], drive_left[fine_step, fine_item]
+            jnp.broadcast_to(fine_item % 2, (1, 1)) == 0,
+            jnp.where(low, from_right, from_left),
+            turned(jnp.where(low, from_left, from_right)),
         )
         rhs_own = decay_now[0:1, :] * own.astype(F32) + drive_at * drive[
             fine_step, fine_item
@@ -396,7 +477,6 @@
                 turn < 9,
             ),
         )
-        fine = jnp.logical_and(middle, item == 1)
         out_slot = jnp.where(
             early,
             jnp.where(last_early, CHAIN + 1, item),
@@ -445,6 +525,25 @@
 
         def one(item, inner):
             job(turn, item)
+
+            @pl.when(jnp.logical_and(turn < 3, item == 1))
+            def _():
+                fill(turn + 1)
+                send_drive(turn + 1)
+
+            @pl.when(
+                jnp.logical_and(
+                    jnp.logical_and(turn == GATED, item == 3), window % 2 == 0
+                )
+            )
+            def _():
+                pl.semaphore_signal(
+                    gate,
+                    inc=1,
+                    device_id={"tm": window + 1, "space": place},
+                    device_id_type=MESH,
+                )
+
             return inner
 
         lax.fori_loop(begin, jobs, one, 0)
@@ -464,32 +563,22 @@
     steps = forcing.shape[0]
     spaces = lax.axis_size("space")
     windows = lax.axis_size("tm")
-    grow = ROWS - width
-    inverses = jnp.pad(
-        jnp.concatenate([block_inv, coarse_inv], axis=0), ((0, 0), (0, grow), (0, grow))
-    )
-    unit = jnp.eye(ROWS, dtype=BF)[None]
-    faces = jnp.concatenate([jnp.pad(-coupling, ((0, 0), (0, grow), (0, grow))), unit], axis=0)
-    faces = faces.transpose(1, 0, 2).reshape(ROWS, DEPTH)
-    meta = jnp.concatenate(
-        [
-            send_index.astype(F32)[None],
-            damping[None],
-            jnp.broadcast_to(etype.astype(F32)[:, None], (1, LANES)),
-            jnp.zeros((5, LANES), F32),
-            conn.astype(F32),
-            jnp.zeros((2, LANES), F32),
-        ],
-        axis=0,
-    )
     vmem = pl.BlockSpec(memory_space=pltpu.VMEM)
+    far = pl.BlockSpec(memory_space=pl.ANY)
     dma = pltpu.SemaphoreType.DMA
     return pl.pallas_call(
         functools.partial(kernel, spaces, windows),
         out_shape=jax.ShapeDtypeStruct((steps, width, LANES), BF),
-        in_specs=[vmem] * 5,
+        in_specs=[far, far, vmem, far, far, far, vmem, vmem, vmem],
         out_specs=vmem,
         scratch_shapes=[
+            pltpu.VMEM((width, LANES), BF),
+            pltpu.VMEM((steps, width, LANES), BF),
+            pltpu.VMEM((4, width, width), BF),
+            pltpu.VMEM((FACES, width, width), BF),
+            pltpu.VMEM((FACES + 4, ROWS, ROWS), BF),
+            pltpu.VMEM((ROWS, DEPTH), BF),
+            pltpu.VMEM((16, LANES), F32),
             pltpu.VMEM((2, 8, 2, ROWS, LANES), BF),
             pltpu.VMEM((2, 8, 4, ROWS, LANES), BF),
             pltpu.VMEM((4 * LANES, 13 * LANES), BF),
@@ -501,11 +590,13 @@
             pltpu.VMEM((2, 8, LANES), F32),
             pltpu.VMEM((4, 4, ROWS, LANES), BF),
             pltpu.VMEM((4, 4, ROWS, LANES), BF),
-            pltpu.VMEM((4, 4, ROWS, LANES), BF),
-            pltpu.VMEM((4, 4, ROWS, LANES), BF),
+            pltpu.VMEM((2, 4, 2, ROWS, LANES), BF),
+            pltpu.VMEM((4, 2, ROWS, LANES), BF),
+            pltpu.VMEM((4, 2, ROWS, LANES), BF),
             pltpu.VMEM((5, ROWS, 2 * LANES), BF),
             pltpu.VMEM((16, LANES), F32),
             pltpu.VMEM((16, LANES), F32),
+            dma((5,)),
             dma((2, 8, 4)),
             dma((2, 8, 4)),
             dma((2,)),
@@ -514,11 +605,22 @@
             dma((2,)),
             dma((4, 2)),
             dma((4, 2)),
+            pltpu.SemaphoreType.REGULAR,
         ],
         compiler_params=pltpu.CompilerParams(
             collective_id=0, has_side_effects=True, vmem_limit_bytes=48 << 20
         ),
-    )(initial, forcing, meta, inverses, faces)
+    )(
+        initial,
+        forcing,
+        damping[None],
+        block_inv,
+        coarse_inv,
+        coupling,
+        etype[None],
+        send_index[None],
+        conn,
+    )
 
 
 def solution(mesh):

time: 158 us -> 138 us (0.87)
  Pallas kernels: 151 us -> 134 us
  local copies, waits for them, and re-layouts: 6.08 us -> 3.7 us
    pallas_call x1, Pallas kernels: 151 us -> 134 us  [shards(): pl.pallas_call(functools.partial(kernel, spaces, windows), out_shape=jax....]
    unnamed x17 -> x15, local copies, waits for them, and re-layouts: 4.5 us -> 2.82 us
where the time goes in v2:
time: 138 us
  Pallas kernels  134 us (97%)
  local copies, waits for them, and re-layouts  3.7 us (3%)
    pallas_call x1, Pallas kernels, shards(): pl.pallas_call(functools.partial(kernel, spaces, windows), out_shape=jax....  134 us
    unnamed x15, local copies, waits for them, and re-layouts  2.82 us

profile of v2, /device:TPU:71, one launch (start us, length us, event | category | flops | bytes accessed | tf_op | source)
XLA Modules:
  0.0 138.1 jit_solution(13653600041115533432)
XLA Ops:
  0.0 0.0 copy-start.5
  0.7 0.9 copy.11.block_in
  1.6 0.9 copy.12.coarse_in
  2.6 0.0 copy-done.5
  2.6 0.0 copy-start
  2.6 0.0 copy-start.1
  2.6 0.0 copy-start.2
  2.6 0.0 copy-start.3
  2.6 0.0 copy-start.4
  2.6 0.1 copy.10.forcing_in
  2.8 0.8 copy-done
  3.6 0.0 copy-done.1
  3.6 0.0 copy-done.2
  3.6 0.0 copy-done.3
  3.6 0.0 copy-done.4
  3.6 133.6 %shard_map.91 = bf16[16,135,128]{2,1,0:T(8,128)(2,1)S(1)} custom-call(bf16[135,128]{1,0:T(8,128)(2,1)S(1)} %copy-done.1, bf16[16,135,128]{2,1,0:T(8,128)(2,1)S(1)} %copy.10.forcing_in, f32[1,128]{1,0:T(1,128)S(1)} %bitcast.4, bf16[2,135,135]{2,1,0:T(8,128)(2,1)S(1)} %copy.11.block_in, bf16[2,135,135]{2,1,0:T(8,128)(2,1)S(1)} %copy.12.coarse_in, ...), custom_call_target="tpu_custom_call" | custom-call | tf_op jit(solution)/shard_map/pallas_call | solution.py:569
  137.2 0.9 copy.13
Async XLA Ops:
  0.0 2.6 %copy-start.5 = (bf16[16,135,128]{2,0,1:T(8,128)(2,1)S(1)}, bf16[16,135,128]{2,0,1:T(8,128)(2,1)}, u32[]{:S(2)}) copy-start(bf16[16,135,128]{2,0,1:T(8,128)(2,1)} %param.10) | copy-start | bytes 1658884
  2.6 1.0 copy-start
  2.6 1.0 copy-start.1
  2.6 1.0 copy-start.2
  2.6 1.0 copy-start.3
  2.6 1.0 copy-start.4

commit v3 on v2

--- a/solution.py
+++ b/solution.py
@@ -36,8 +36,7 @@
     initial_in,
     forcing_in,
     damping,
-    block_in,
-    coarse_in,
+    inverse_in,
     coupling_in,
     etype,
     send_index,
@@ -58,6 +57,7 @@
     mats,
     own_mats,
     stacked,
+    waiting,
     decay,
     drive,
     drive_sel,
@@ -88,9 +88,8 @@
     loads = [
         pltpu.make_async_copy(initial_in, initial, load_sem.at[0]),
         pltpu.make_async_copy(forcing_in, forcing, load_sem.at[1]),
-        pltpu.make_async_copy(block_in, inverse.at[0:2], load_sem.at[2]),
-        pltpu.make_async_copy(coarse_in, inverse.at[2:4], load_sem.at[3]),
-        pltpu.make_async_copy(coupling_in, coupling, load_sem.at[4]),
+        pltpu.make_async_copy(inverse_in, inverse, load_sem.at[2]),
+        pltpu.make_async_copy(coupling_in, coupling, load_sem.at[3]),
     ]
     for load in loads:
         load.start()
@@ -301,6 +300,9 @@
         gather_two[:, here] = onehot(code, two_own[face : face + 1, :])
         gather_two[:, after] = onehot(code, two_listed[face : face + 1, :])
 
+    for step in range(1, 4):
+        fill(step)
+
     for side in range(2):
         @pl.when(inside((-1, 1)[side]))
         def _():
@@ -380,14 +382,6 @@
         )
         handed = jnp.logical_and(turn == 4, item == 0)
 
-        @pl.when(fresh)
-        def _():
-            await_state(parity, slot)
-
-        @pl.when(jnp.logical_and(fresh, jnp.logical_not(handed)))
-        def _():
-            await_sent(parity, slot)
-
         @pl.when(handed)
         def _():
             for part in range(2):
@@ -412,9 +406,6 @@
 
         own = source[parity, slot, 0]
         listed = source[parity, slot, 1]
-        outer = jnp.where(low, received[parity, slot, 3], received[parity, slot, 2])
-        near = jnp.concatenate([received[parity, slot, 0], own], axis=1)
-        far = jnp.concatenate([received[parity, slot, 1], outer], axis=1)
         decay_now = decay[op]
         from_left = drive_left[fine_step, fine_item // 2]
         from_right = drive_right[fine_step, fine_item // 2]
@@ -440,14 +431,24 @@
                 ]
 
         tail = slice(FACES * ROWS, DEPTH)
+        stacked[tail, 0:LANES] = rhs_own.astype(BF)
+        waiting[0] = rhs_listed.astype(BF)
+        waiting[1] = (drive_at * drive_beside.astype(F32)).astype(BF)
+
+        @pl.when(fresh)
+        def _():
+            await_state(parity, slot)
+
+        outer = jnp.where(low, received[parity, slot, 3], received[parity, slot, 2])
+        near = jnp.concatenate([received[parity, slot, 0], own], axis=1)
+        far = jnp.concatenate([received[parity, slot, 1], outer], axis=1)
         gathered = matmul(near, gather_one[0 : 2 * LANES, :]) + matmul(
             far, gather_one[2 * LANES :, :]
         )
         stack(gathered)
-        stacked[tail, 0:LANES] = rhs_own.astype(BF)
         rhs_beside = decay_now[1:2, :] * gathered[
             :, 2 * FACES * LANES :
-        ] + drive_at * drive_beside.astype(F32)
+        ] + waiting[1].astype(F32)
         stacked[tail, LANES : 2 * LANES] = rhs_beside.astype(BF)
         kinds = jnp.concatenate([decay[0, 3:4, :], decay[0, 4:5, :]], axis=1)
         once = jnp.where(
@@ -457,7 +458,7 @@
         ).astype(BF)
 
         stack(matmul(once, gather_two[...]))
-        stacked[tail, LANES : 2 * LANES] = rhs_listed.astype(BF)
+        stacked[tail, LANES : 2 * LANES] = waiting[0]
         plus = residual[jnp.where(coarse, turn - 4, CHAIN)].astype(F32)
         twice = (matmul(own_mats[op], stacked[...]) + plus).astype(BF)
 
@@ -515,6 +516,10 @@
         def _():
             out[out_index] = twice[0:width, 0:LANES]
 
+        @pl.when(jnp.logical_and(fresh, jnp.logical_not(handed)))
+        def _():
+            await_sent(parity, slot)
+
     def round_of(turn, carry):
         early = turn < 4
         middle = jnp.logical_and(turn >= 4, turn < 8)
@@ -526,9 +531,8 @@
         def one(item, inner):
             job(turn, item)
 
-            @pl.when(jnp.logical_and(turn < 3, item == 1))
+            @pl.when(jnp.logical_and(turn < 3, item == 0))
             def _():
-                fill(turn + 1)
                 send_drive(turn + 1)
 
             @pl.when(
@@ -569,7 +573,7 @@
     return pl.pallas_call(
         functools.partial(kernel, spaces, windows),
         out_shape=jax.ShapeDtypeStruct((steps, width, LANES), BF),
-        in_specs=[far, far, vmem, far, far, far, vmem, vmem, vmem],
+        in_specs=[far, far, vmem, far, far, vmem, vmem, vmem],
         out_specs=vmem,
         scratch_shapes=[
             pltpu.VMEM((width, LANES), BF),
@@ -587,6 +591,7 @@
             pltpu.VMEM((4, ROWS, DEPTH), BF),
             pltpu.VMEM((2, ROWS, DEPTH), BF),
             pltpu.VMEM((DEPTH, 2 * LANES), BF),
+            pltpu.VMEM((2, ROWS, LANES), BF),
             pltpu.VMEM((2, 8, LANES), F32),
             pltpu.VMEM((4, 4, ROWS, LANES), BF),
             pltpu.VMEM((4, 4, ROWS, LANES), BF),
@@ -596,7 +601,7 @@
             pltpu.VMEM((5, ROWS, 2 * LANES), BF),
             pltpu.VMEM((16, LANES), F32),
             pltpu.VMEM((16, LANES), F32),
-            dma((5,)),
+            dma((4,)),
             dma((2, 8, 4)),
             dma((2, 8, 4)),
             dma((2,)),
@@ -614,8 +619,7 @@
         initial,
         forcing,
         damping[None],
-        block_inv,
-        coarse_inv,
+        jnp.concatenate([block_inv, coarse_inv], axis=0),
         coupling,
         etype[None],
         send_index[None],

time: 138 us -> 135 us (0.978)
  Pallas kernels: 134 us -> 131 us
    pallas_call x1, Pallas kernels: 134 us -> 131 us  [shards(): pl.pallas_call(functools.partial(kernel, spaces, windows), out_shape=jax....]
    unnamed x15 -> x17, local copies, waits for them, and re-layouts: 2.82 us -> 2.1 us
where the time goes in v3:
time: 135 us
  Pallas kernels  131 us (97%)
  local copies, waits for them, and re-layouts  2.97 us (2%)
    pallas_call x1, Pallas kernels, shards(): pl.pallas_call(functools.partial(kernel, spaces, windows), out_shape=jax....  131 us

profile of v3, /device:TPU:71, one launch (start us, length us, event | category | flops | bytes accessed | tf_op | source)
XLA Modules:
  0.0 134.7 jit_solution(1047332609738382841)
XLA Ops:
  0.7 0.0 copy-start.6
  0.7 0.0 copy-start.5
  0.7 1.0 copy.10
  1.7 0.0 copy-done.6
  1.7 0.1 pad_maximum_fusion.inverse_in
  1.8 0.1 copy-done.5
  1.9 0.0 copy-start
  1.9 0.0 copy-start.1
  1.9 0.0 copy-start.2
  1.9 0.0 copy-start.3
  1.9 0.0 copy-start.4
  1.9 0.1 copy.12.forcing_in
  2.0 0.8 copy-done
  2.9 0.0 copy-done.1
  2.9 0.0 copy-done.2
  2.9 0.0 copy-done.3
  2.9 0.0 copy-done.4
  2.9 130.9 %shard_map.91 = bf16[16,135,128]{2,1,0:T(8,128)(2,1)S(1)} custom-call(bf16[135,128]{1,0:T(8,128)(2,1)S(1)} %copy-done.1, bf16[16,135,128]{2,1,0:T(8,128)(2,1)S(1)} %copy.12.forcing_in, f32[1,128]{1,0:T(1,128)S(1)} %bitcast.4, bf16[4,135,135]{2,1,0:T(8,128)(2,1)S(1)} %pad_maximum_fusion.inverse_in, bf16[6,135,135]{2,1,0:T(8,128)(2,1)S(1)} %copy-done, ...), custom_call_target="tpu_custom_call" | custom-call | tf_op jit(solution)/shard_map/pallas_call | solution.py:573
  133.8 0.9 copy.13
  (1 shorter events, 0.0 us)
Async XLA Ops:
  0.7 1.0 copy-start.6
  0.7 1.2 copy-start.5
  1.9 1.0 copy-start
  1.9 1.0 copy-start.1
  1.9 1.0 copy-start.2
  1.9 1.0 copy-start.3
  1.9 1.0 copy-start.4

commit v4 on v3

--- a/solution.py
+++ b/solution.py
@@ -16,6 +16,7 @@
 DEPTH = (FACES + 1) * ROWS
 CHAIN = 4
 GATED = 1
+HELD = 3
 OFFSETS = (1, -1, 2, -2)
 MESH = pl.DeviceIdType.MESH
 BF = jnp.bfloat16
@@ -364,23 +365,31 @@
         send_drive(0)
 
 
-    def job(turn, item):
+    def held(part_now):
+        return jnp.where(jnp.logical_and(part_now > 1, window < windows - 1), HELD, 0)
+
+    def job(turn, order):
         early = turn < 4
-        middle = jnp.logical_and(turn >= 4, turn < 8)
         ending = jnp.logical_and(turn == 7, window == windows - 1)
-        fine = jnp.logical_and(middle, item == jnp.where(ending, 0, 1))
-        coarse = jnp.logical_and(middle, jnp.logical_not(fine))
+        swapped = jnp.where(ending, jnp.where(order < 2, 1 - order, order), order)
+        part_now = jnp.where(early, 0, swapped)
+        coarse = jnp.logical_and(jnp.logical_not(early), part_now == 0)
+        fine = part_now > 0
+        shared = jnp.logical_or(coarse, part_now == 1)
+        item = jnp.where(
+            early, order, jnp.where(coarse, turn - 4, turn - 3 - part_now - held(part_now))
+        )
         first = window == 0
-        parity = jnp.where(middle, 0, turn % 2)
-        slot = jnp.where(middle, turn, item)
+        parity = jnp.where(early, turn % 2, jnp.where(part_now == 3, 1, 0))
+        slot = jnp.where(shared, turn, item)
         op = jnp.where(coarse, 1, 0)
 
         fresh = jnp.where(
             early,
             jnp.logical_or(turn >= 1, jnp.logical_and(item == 0, first)),
-            jnp.logical_not(jnp.logical_and(middle, item == 1)),
-        )
-        handed = jnp.logical_and(turn == 4, item == 0)
+            jnp.logical_or(jnp.logical_not(shared), order == 0),
+        )
+        handed = jnp.logical_and(turn == 4, order == 0)
 
         @pl.when(handed)
         def _():
@@ -398,10 +407,8 @@
                 def _():
                     drive_copy(turn, side).wait_send()
 
-        fine_step = jnp.where(early, turn, jnp.where(middle, 0, turn - 7))
-        fine_item = jnp.where(middle, turn - 4, item)
-        drive_step = jnp.where(coarse, 4, fine_step)
-        drive_item = jnp.where(coarse, 0, fine_item)
+        fine_step = jnp.where(early, turn, jnp.where(coarse, 0, part_now - 1))
+        fine_item = item
         drive_at = jnp.where(coarse, 0.0, 1.0)
 
         own = source[parity, slot, 0]
@@ -459,7 +466,7 @@
 
         stack(matmul(once, gather_two[...]))
         stacked[tail, LANES : 2 * LANES] = waiting[0]
-        plus = residual[jnp.where(coarse, turn - 4, CHAIN)].astype(F32)
+        plus = residual[jnp.where(coarse, item, CHAIN)].astype(F32)
         twice = (matmul(own_mats[op], stacked[...]) + plus).astype(BF)
 
         leading = jnp.logical_and(first, item == 0)
@@ -472,22 +479,18 @@
         sending = jnp.where(
             early,
             jnp.logical_or(turn < 3, leading),
-            jnp.where(
-                coarse,
-                jnp.logical_or(turn < 7, window < windows - 1),
-                turn < 9,
-            ),
+            jnp.where(coarse, jnp.logical_or(turn < 7, window < windows - 1), part_now < 3),
         )
         out_slot = jnp.where(
             early,
             jnp.where(last_early, CHAIN + 1, item),
-            jnp.where(
-                coarse,
-                jnp.where(turn == 7, CHAIN, turn + 1),
-                jnp.where(fine, turn - 4, item),
-            ),
-        )
-        out_parity = jnp.where(jnp.logical_or(middle, last_early), 0, (turn + 1) % 2)
+            jnp.where(coarse, jnp.where(turn == 7, CHAIN, turn + 1), item),
+        )
+        out_parity = jnp.where(
+            early,
+            jnp.where(last_early, 0, (turn + 1) % 2),
+            jnp.where(part_now == 2, 1, 0),
+        )
         leaving = jnp.logical_and(coarse, turn == 7)
         target = jnp.where(leaving, window + 1, window)
 
@@ -505,11 +508,7 @@
         out_index = jnp.where(
             early,
             turn,
-            jnp.where(
-                coarse,
-                COARSEN * (turn - 4) + COARSEN - 1,
-                jnp.where(fine, COARSEN * (turn - 4), COARSEN * item + turn - 7),
-            ),
+            COARSEN * item + jnp.where(coarse, COARSEN - 1, part_now - 1),
         )
 
         @pl.when(jnp.logical_or(jnp.logical_not(early), leading))
@@ -522,14 +521,23 @@
 
     def round_of(turn, carry):
         early = turn < 4
-        middle = jnp.logical_and(turn >= 4, turn < 8)
-        begin = jnp.where(jnp.logical_and(turn >= 8, window == 0), 1, 0)
-        jobs = jnp.where(
-            middle, jnp.where(jnp.logical_and(turn == 4, window == 0), 0, 2), 4
-        )
+        begin = jnp.where(turn >= 8, 2, 0)
 
         def one(item, inner):
-            job(turn, item)
+            interval = turn - 3 - item - held(item)
+            counted = jnp.logical_and(
+                jnp.logical_and(interval >= 0, interval <= 3),
+                jnp.logical_or(window > 0, interval > 0),
+            )
+            stepped = jnp.where(
+                item == 0,
+                jnp.logical_or(window > 0, turn > 4),
+                counted,
+            )
+
+            @pl.when(jnp.logical_or(early, stepped))
+            def _():
+                job(turn, item)
 
             @pl.when(jnp.logical_and(turn < 3, item == 0))
             def _():
@@ -550,10 +558,10 @@
 
             return inner
 
-        lax.fori_loop(begin, jobs, one, 0)
+        lax.fori_loop(begin, 4, one, 0)
         return carry
 
-    lax.fori_loop(0, 10, round_of, 0)
+    lax.fori_loop(0, jnp.where(window < windows - 1, 10 + HELD, 10), round_of, 0)
 
     @pl.when(window < windows - 1)
     def _():

time: 135 us -> 134 us (level)
  no operation moved by 1% of the time
where the time goes in v4:
time: 134 us
  Pallas kernels  130 us (97%)
  local copies, waits for them, and re-layouts  2.97 us (2%)
    pallas_call x1, Pallas kernels, shards(): pl.pallas_call(functools.partial(kernel, spaces, windows), out_shape=jax....  130 us

profile of v4, /device:TPU:71, one launch (start us, length us, event | category | flops | bytes accessed | tf_op | source)
XLA Modules:
  0.0 133.8 jit_solution(17676653693133174258)
XLA Ops:
  0.7 0.0 copy-start.6
  0.7 0.0 copy-start.5
  0.7 1.0 copy.10
  1.7 0.0 copy-done.6
  1.7 0.1 pad_maximum_fusion.inverse_in
  1.8 0.1 copy-done.5
  1.9 0.0 copy-start
  1.9 0.0 copy-start.1
  1.9 0.0 copy-start.2
  1.9 0.0 copy-start.3
  1.9 0.0 copy-start.4
  1.9 0.1 copy.12.forcing_in
  2.0 0.8 copy-done
  2.9 0.0 copy-done.1
  2.9 0.0 copy-done.2
  2.9 0.0 copy-done.3
  2.9 0.0 copy-done.4
  2.9 130.1 %shard_map.91 = bf16[16,135,128]{2,1,0:T(8,128)(2,1)S(1)} custom-call(bf16[135,128]{1,0:T(8,128)(2,1)S(1)} %copy-done.1, bf16[16,135,128]{2,1,0:T(8,128)(2,1)S(1)} %copy.12.forcing_in, f32[1,128]{1,0:T(1,128)S(1)} %bitcast.4, bf16[4,135,135]{2,1,0:T(8,128)(2,1)S(1)} %pad_maximum_fusion.inverse_in, bf16[6,135,135]{2,1,0:T(8,128)(2,1)S(1)} %copy-done, ...), custom_call_target="tpu_custom_call" | custom-call | tf_op jit(solution)/shard_map/pallas_call | solution.py:581
  132.9 0.9 copy.13
  (1 shorter events, 0.0 us)
Async XLA Ops:
  0.7 1.0 copy-start.6
  0.7 1.2 copy-start.5
  1.9 1.0 copy-start
  1.9 1.0 copy-start.1
  1.9 1.0 copy-start.2
  1.9 1.0 copy-start.3
  1.9 1.0 copy-start.4

commit v5 on v4

--- a/solution.py
+++ b/solution.py
@@ -440,7 +440,7 @@
         tail = slice(FACES * ROWS, DEPTH)
         stacked[tail, 0:LANES] = rhs_own.astype(BF)
         waiting[0] = rhs_listed.astype(BF)
-        waiting[1] = (drive_at * drive_beside.astype(F32)).astype(BF)
+        waiting[1] = drive_beside * drive_at.astype(BF)
 
         @pl.when(fresh)
         def _():

time: 134 us -> 134 us (level)
  no operation moved by 1% of the time
where the time goes in v5:
time: 134 us; the launch traced here: 133 us
  Pallas kernels  130 us (97%)
  local copies, waits for them, and re-layouts  2.97 us (2%)
    pallas_call x1, Pallas kernels, shards(): pl.pallas_call(functools.partial(kernel, spaces, windows), out_shape=jax....  130 us

profile of v5, /device:TPU:71, one launch (start us, length us, event | category | flops | bytes accessed | tf_op | source)
XLA Modules:
  0.0 133.5 jit_solution(17875554953127906303)
XLA Ops:
  0.7 0.0 copy-start.6
  0.7 0.0 copy-start.5
  0.7 1.0 copy.10
  1.7 0.0 copy-done.6
  1.7 0.1 pad_maximum_fusion.inverse_in
  1.8 0.1 copy-done.5
  1.9 0.0 copy-start
  1.9 0.0 copy-start.1
  1.9 0.0 copy-start.2
  1.9 0.0 copy-start.3
  1.9 0.0 copy-start.4
  1.9 0.1 copy.12.forcing_in
  2.0 0.8 copy-done
  2.9 0.0 copy-done.1
  2.9 0.0 copy-done.2
  2.9 0.0 copy-done.3
  2.9 0.0 copy-done.4
  2.9 129.7 %shard_map.91 = bf16[16,135,128]{2,1,0:T(8,128)(2,1)S(1)} custom-call(bf16[135,128]{1,0:T(8,128)(2,1)S(1)} %copy-done.1, bf16[16,135,128]{2,1,0:T(8,128)(2,1)S(1)} %copy.12.forcing_in, f32[1,128]{1,0:T(1,128)S(1)} %bitcast.4, bf16[4,135,135]{2,1,0:T(8,128)(2,1)S(1)} %pad_maximum_fusion.inverse_in, bf16[6,135,135]{2,1,0:T(8,128)(2,1)S(1)} %copy-done, ...), custom_call_target="tpu_custom_call" | custom-call | tf_op jit(solution)/shard_map/pallas_call | solution.py:581
  132.6 0.9 copy.13
  (1 shorter events, 0.0 us)
Async XLA Ops:
  0.7 1.0 copy-start.6
  0.7 1.2 copy-start.5
  1.9 1.0 copy-start
  1.9 1.0 copy-start.1
  1.9 1.0 copy-start.2
  1.9 1.0 copy-start.3
  1.9 1.0 copy-start.4
